TPU v7x, 256 devices: a whole 4x4x8 slice. The times are simulated.
256 devices in a mesh: grp: 16 (over z_lo, x), own: 16 (over z_hi, y, core).
Axes of the slice: x: 4, y: 4, z: 8 (z_hi: 2, z_lo: 4; z = z_hi * 4 + z_lo), core: 2. Of those that a mesh axis runs over, the one named last changes fastest.
Arguments:
- vectors: float32 [16, 64, 2048], P('own'), may hold values from -6 to 6
- tiles: float32 [16, 16, 128, 128, 128], P('grp', 'own'), may hold values from -0.046875 to 0.046875
- tile_rows: int32 [16, 16, 128], P('grp', 'own'), may hold values from 0 to 15
- tile_cols: int32 [16, 16, 128], P('grp', 'own'), may hold values from 0 to 63
- tile_counts: int32 [16, 16], P('grp', 'own'), may hold values from 16 to 128, as said below
- matchings: int32 [16, 3], P('grp'), may hold values from 1 to 15, as said below
Outputs:
- products: float32 [16, 64, 2048], P('own', None, 'grp')
Inputs may be any that keep to these rules, and one draw needn't show every extreme that they name: `tile_counts`: the largest value 128 is held by some device in every draw. Each row holds 3 different values; matching j of part g pairs owner o with owner o XOR matchings[g, j].
All inputs are finite; a program needn't handle non-finite values.
Results may differ from a plain program's by a relative error of at most 0.0003.
Values sent between devices are 32-bit elements; how exact they have to be, the bound alone decides.
No kernel may reach another device: no remote copies, remote signals or barrier semaphores. Data moves between devices by JAX's collectives and lax.ppermute only.
A program may use at most 64 MiB of HBM per device.

v0:
```python
import jax
import jax.numpy as jnp
from jax import lax
from jax.experimental import pallas as pl
from jax.experimental.pallas import tpu as pltpu
from jax.sharding import Mesh, PartitionSpec as P

ZLO, X, ZHI, Y, CORE = 4, 4, 2, 4, 2
YC = Y * CORE
OWN = ZHI * YC
FAN = X * YC
GRP_AXES = ("zlo", "x")
OWN_AXES = ("zhi", "y", "core")
FAN_AXES = ("x", "y", "core")
YC_AXES = ("y", "core")


REGIONS = 4
SUB = 8
LANE = 128
CHUNK = 16
GROUP = 8
SMALL = 8 << 20
LARGE = 56 << 20
ROWS = 52 << 20

VMEM = pl.BlockSpec(memory_space=pltpu.VMEM)
SMEM = pl.BlockSpec(memory_space=pltpu.SMEM)
HBM = pl.BlockSpec(memory_space=pltpu.HBM)

BY_COLS = (((1,), (0,)), ((), ()))
BY_ROWS = (((1,), (1,)), ((), ()))


def halves(value):
    high = value.astype(jnp.bfloat16)
    return high, (value - high.astype(jnp.float32)).astype(jnp.bfloat16)


def product(pair, high, low, dims):
    both = jnp.concatenate([high, low], axis=1 if dims is BY_COLS else 0)
    wide = lax.dot_general(pair, both, dims, preferred_element_type=jnp.float32)
    count = pair.shape[0] // 2
    return wide[:count, :LANE] + wide[count:, :LANE] + wide[:count, LANE:]


def pieces_kernel(x_ref, yc_ref, own_ref, out_ref, held, sems):
    copies = []
    for zlo in range(ZLO):
        col = pl.multiple_of((zlo * X + x_ref[0]) * LANE, LANE)
        copies.append(
            pltpu.make_async_copy(own_ref.at[:, pl.ds(col, LANE)], held.at[zlo], sems.at[zlo])
        )
    for copy in copies:
        copy.start()
    for copy in copies:
        copy.wait()
    for step in range(YC):
        row = pl.multiple_of((yc_ref[0] ^ step) * SUB, SUB)
        for zlo in range(ZLO):
            out_ref[step, zlo] = held[zlo, pl.ds(row, SUB)]


def pair_kernel(near_ref, other_ref, *outs):
    for step in range(YC):
        outs[step][0] = near_ref[step]
        outs[step][1] = other_ref[step]


def route_kernel(x_ref, yc_ref, m0, m1, m2, m3, *refs):
    pieces, out_ref, held = refs[:YC], refs[YC], refs[YC + 1]
    for step in range(YC):
        for zhi in range(ZHI):
            held[zhi * YC + step] = pieces[step][zhi]
    for step, masks in enumerate((m0, m1, m2, m3)):
        base = lax.rem(x_ref[0] + step, X) * YC
        for slot in range(REGIONS - 1):
            mask = masks[0, slot]
            for part in range(YC):
                out_ref[base + part, slot] = held[(part ^ yc_ref[0]) ^ mask]


def collect_kernel(x_ref, yc_ref, zlo_ref, m0, m1, m2, m3, parts_ref, near_ref, other_ref, sums):
    sums[...] = jnp.zeros_like(sums)
    for step, masks in enumerate((m0, m1, m2, m3)):
        base = lax.rem(x_ref[0] + step, X) * YC
        for slot in range(REGIONS - 1):
            mask = masks[0, slot]
            for part in range(YC):
                owner = (part ^ yc_ref[0]) ^ mask
                for zlo in range(ZLO):
                    sums[zlo, owner] += parts_ref[base + part, slot, zlo]
    for step in range(ZLO):
        zlo = zlo_ref[0] ^ step
        near_ref[step] = sums[zlo, :YC]
        other_ref[step] = sums[zlo, YC:]


def add_zhi_kernel(a_ref, b_ref, *outs):
    for step in range(ZLO):
        outs[step][...] = a_ref[step] + b_ref[step]


def add_zlo_kernel(a_ref, b_ref, c_ref, d_ref, *outs):
    for step in range(YC):
        outs[step][...] = (a_ref[step] + b_ref[step]) + (c_ref[step] + d_ref[step])


def final_kernel(yc_ref, rows_ref, *refs):
    parts, out_ref = refs[:YC], refs[YC]
    for step in range(YC):
        at = pl.ds(pl.multiple_of((yc_ref[0] ^ step) * SUB, SUB), SUB)
        total = parts[step][...]
        for group in range(rows_ref.shape[0]):
            total = total + rows_ref[group, at]
        out_ref[at] = total


def load_table(table, base, blocks, get, vecs):
    for block in range(blocks):
        high, low = halves(get(block))
        table[base + block, :vecs] = high
        table[base + block, vecs:] = low


def fetch(tiles, held, sems):
    copies = [
        pltpu.make_async_copy(
            tiles.at[pl.ds(i * CHUNK, CHUNK)], held.at[pl.ds(i * CHUNK, CHUNK)], sems.at[i]
        )
        for i in range(held.shape[0] // CHUNK)
    ]
    for copy in copies:
        copy.start()
    return copies


def each_group(copies, live, group):
    for i, copy in enumerate(copies):
        copy.wait()
        here = jnp.clip(live - i * CHUNK, 0, CHUNK)
        full = here // GROUP

        def several(step, carry, i=i):
            group(i * CHUNK + step * GROUP, GROUP)
            return carry

        def single(step, carry, i=i):
            group(i * CHUNK + step, 1)
            return carry

        lax.fori_loop(0, full, several, 0)
        lax.fori_loop(full * GROUP, here, single, 0)


def columns_kernel(rows, cols, count, tiles, own_ref, out_ref, self_ref, held, table, sums, sems):
    copies = fetch(tiles, held, sems)
    sums[...] = jnp.zeros_like(sums)
    vecs = own_ref.shape[0]
    blocks = own_ref.shape[1] // LANE
    load_table(table, 0, blocks, lambda b: own_ref[:, b * LANE : (b + 1) * LANE], vecs)

    def group(first, size):
        done = []
        for k in range(size):
            high, low = halves(held[first + k])
            done.append(product(table[rows[first + k]], high, low, BY_COLS))
        for k in range(size):
            col = cols[first + k]
            sums[col] += done[k]

    each_group(copies, count[0], group)
    self_ref[...] = sums[:blocks]
    for slot in range(REGIONS - 1):
        for block in range(blocks):
            zlo, x = divmod(block, X)
            value = sums[(slot + 1) * blocks + block]
            for part in range(YC):
                out_ref[x * YC + part, slot, zlo] = value[part * SUB : (part + 1) * SUB]


def rows_kernel(rows, cols, count, tiles, own_ref, far_ref, self_ref, sums, held, table, sems):
    copies = fetch(tiles, held, sems)
    sums[...] = self_ref[...]
    vecs = own_ref.shape[0]
    blocks = own_ref.shape[1] // LANE
    load_table(table, 0, blocks, lambda b: own_ref[:, b * LANE : (b + 1) * LANE], vecs)
    for slot in range(REGIONS - 1):

        def far(b, slot=slot):
            return jnp.concatenate(
                [far_ref[b % X * YC + part, slot, b // X] for part in range(YC)], axis=0
            )

        load_table(table, (slot + 1) * blocks, blocks, far, vecs)

    def group(first, size):
        done = []
        for k in range(size):
            high, low = halves(held[first + k])
            done.append(product(table[cols[first + k]], high, low, BY_ROWS))
        for k in range(size):
            row = rows[first + k]
            sums[row] += done[k]

    each_group(copies, count[0], group)


def exchange(value, axes):
    return lax.all_to_all(value, axes, 0, 0, tiled=False)


def local(kernel, outs, specs, scratch=(), limit=None, cost=None):
    outs = [jax.ShapeDtypeStruct(shape, jnp.float32) for shape in outs]
    return pl.pallas_call(
        kernel,
        out_shape=outs,
        in_specs=specs,
        out_specs=[VMEM] * len(outs),
        scratch_shapes=scratch,
        compiler_params=pltpu.CompilerParams(vmem_limit_bytes=limit),
        cost_estimate=cost,
    )


def swaps(arrays, axes, count):
    return [arrays[0]] + [
        lax.ppermute(arrays[step], axes, [(i, i ^ step) for i in range(count)])
        for step in range(1, count)
    ]


def on_device(vectors, tiles, tile_rows, tile_cols, tile_counts, matchings):
    own = vectors[0]
    tile_set = tiles[0, 0]
    vecs, rows_own = own.shape
    slots = tile_set.shape[0]
    blocks = rows_own // LANE
    x, zlo, yc = (
        lax.axis_index(axes).reshape(1).astype(jnp.int32) for axes in ("x", "zlo", YC_AXES)
    )
    ids = (tile_rows[0, 0], tile_cols[0, 0], tile_counts[0])
    piece = (ZLO, SUB, LANE)
    half = pl.CostEstimate(
        flops=slots * 6 * vecs * LANE * LANE, bytes_accessed=tile_set.size * 4, transcendentals=0
    )

    def tile_scratch(operand, result):
        sums = [pltpu.VMEM((result, vecs, LANE), jnp.float32)] if result else []
        return [
            pltpu.VMEM(tile_set.shape, jnp.float32),
            pltpu.VMEM((operand, 2 * vecs, LANE), jnp.bfloat16),
            *sums,
            pltpu.SemaphoreType.DMA((slots // CHUNK,)),
        ]

    whole = (YC, *piece)
    (near,) = local(
        pieces_kernel,
        [whole],
        [SMEM] * 2 + [HBM],
        [pltpu.VMEM((ZLO, vecs, LANE), jnp.float32), pltpu.SemaphoreType.DMA((ZLO,))],
        SMALL,
    )(x, yc, own)
    other = lax.ppermute(near, "zhi", [(0, 1), (1, 0)])
    masks = [matchings] + [
        lax.ppermute(matchings, "x", [(i, (i - step) % X) for i in range(X)])
        for step in range(1, X)
    ]
    parts, mine = local(
        columns_kernel,
        [(FAN, REGIONS - 1, *piece), (blocks, vecs, LANE)],
        [SMEM] * 3 + [HBM, VMEM],
        tile_scratch(blocks, REGIONS * blocks),
        LARGE,
        half,
    )(*ids, tile_set, own)
    parts = exchange(parts, FAN_AXES)
    pieces = local(pair_kernel, [(ZHI, *piece)] * YC, [VMEM] * 2, limit=SMALL)(near, other)
    pieces = swaps(pieces, YC_AXES, YC)
    (wanted,) = local(
        route_kernel,
        [(FAN, REGIONS - 1, *piece)],
        [SMEM] * 6 + [VMEM] * YC,
        [pltpu.VMEM((OWN, *piece), jnp.float32)],
        SMALL,
    )(x, yc, *masks, *pieces)
    parts, wanted = lax.optimization_barrier((parts, wanted))
    far = exchange(wanted, FAN_AXES)
    spread = (ZLO, YC, SUB, LANE)
    near, other = local(
        collect_kernel,
        [spread] * 2,
        [SMEM] * 7 + [VMEM],
        [pltpu.VMEM((ZLO, OWN, SUB, LANE), jnp.float32)],
        SMALL,
    )(x, yc, zlo, *masks, parts)
    other = lax.ppermute(other, "zhi", [(0, 1), (1, 0)])
    parts = local(add_zhi_kernel, [spread[1:]] * ZLO, [VMEM] * 2, limit=SMALL)(near, other)
    parts = swaps(parts, "zlo", ZLO)
    parts = local(add_zlo_kernel, [spread[2:]] * YC, [VMEM] * ZLO, limit=SMALL)(*parts)
    (rows,) = local(
        rows_kernel,
        [(blocks, vecs, LANE)],
        [SMEM] * 3 + [HBM, VMEM, VMEM, VMEM],
        tile_scratch(REGIONS * blocks, None),
        ROWS,
        half,
    )(*ids, tile_set, own, far, mine)
    rows, *parts = lax.optimization_barrier((rows, *parts))
    rows = exchange(rows, GRP_AXES)
    parts = swaps(parts, YC_AXES, YC)
    (total,) = local(final_kernel, [(vecs, LANE)], [SMEM] + [VMEM] * (1 + YC), limit=SMALL)(
        yc, rows, *parts
    )
    return total[None]


def solution(mesh):
    fine = Mesh(mesh.devices.reshape(ZLO, X, ZHI, Y, CORE), ("zlo", "x", "zhi", "y", "core"))
    return jax.shard_map(
        on_device,
        mesh=fine,
        in_specs=(
            P(OWN_AXES, None, None),
            P(GRP_AXES, OWN_AXES, None, None, None),
            P(GRP_AXES, OWN_AXES, None),
            P(GRP_AXES, OWN_AXES, None),
            P(GRP_AXES, OWN_AXES),
            P(GRP_AXES, None),
        ),
        out_specs=P(OWN_AXES, None, GRP_AXES),
        check_vma=False,
    )
```

profile of v0, /device:TPU:1, one launch (start us, length us, event | category | flops | bytes accessed | tf_op | source)
XLA Modules:
  0.0 108.7 jit_solution(9748773302317449534)
XLA Ops:
  0.7 6.2 %shard_map.64 = (f32[32,3,4,8,128]{4,3,2,1,0:T(8,128)}, f32[16,64,128]{2,1,0:T(8,128)}) custom-call(s32[128]{0:T(128)} %bitcast.14, s32[128]{0:T(128)} %bitcast.16, s32[1]{0:T(128)} %bitcast.9.count, f32[128,128,128]{2,1,0:T(8,128)} %bitcast.18, f32[64,2048]{1,0:T(8,128)} %bitcast.11), custom_call_target="tpu_custom_call" | custom-call | flops 805306368 | bytes 8388608 | tf_op jit(solution)/shard_map/pallas_call | solution.py:270
  6.9 9.4 %all-to-all-start = ((f32[32,3,4,8,128]{4,3,2,1,0:T(8,128)}), f32[32,3,4,8,128]{4,3,2,1,0:T(8,128)S(1)}, u32[]{:S(2)}, u32[]{:S(2)}) async-start(f32[32,3,4,8,128]{4,3,2,1,0:T(8,128)} %get-tuple-element.40), calls=%async_computation | async-start | bytes 3145728 | tf_op jit(solution)/shard_map/all_to_all | solution.py:210
  16.5 6.7 %collective-permute-start.3 = (f32[8,4,8,128]{3,2,1,0:T(8,128)S(1)}, f32[8,4,8,128]{3,2,1,0:T(8,128)S(1)}, u32[]{:S(2)}, u32[]{:S(2)}) collective-permute-start(f32[8,4,8,128]{3,2,1,0:T(8,128)S(1)} %shard_map.65.near_ref), channel_id=1, source_target_pairs={{0,8},{8,0},{1,9},{9,1},{2,10},{10,2},{3,11},{11,3},{4,12},{12,4},... | collective-permute-start | bytes 393224 | tf_op jit(solution)/shard_map/ppermute | solution.py:265
  23.2 3.6 %collective-permute-done.3.other_ref = f32[8,4,8,128]{3,2,1,0:T(8,128)S(1)} collective-permute-done((f32[8,4,8,128]{3,2,1,0:T(8,128)S(1)}, f32[8,4,8,128]{3,2,1,0:T(8,128)S(1)}, u32[]{:S(2)}, u32[]{:S(2)}) %collective-permute-start.3) | collective-permute-done | bytes 131104 | tf_op jit(solution)/shard_map/ppermute | solution.py:265
  26.9 1.0 collective-permute-start.4
  27.9 1.4 %collective-permute-start.5 = (f32[2,4,8,128]{3,2,1,0:T(8,128)S(1)}, f32[2,4,8,128]{3,2,1,0:T(8,128)S(1)}, u32[]{:S(2)}, u32[]{:S(2)}) collective-permute-start(f32[2,4,8,128]{3,2,1,0:T(8,128)S(1)} %get-tuple-element.43), channel_id=1, source_target_pairs={{0,2},{1,3},{2,0},{3,1},{4,6},{5,7},{6,4},{7,5},{8,10},{9,11},{10,... | collective-permute-start | bytes 98312 | tf_op jit(solution)/shard_map/ppermute | solution.py:228
  29.2 1.2 %collective-permute-start.2 = (s32[1,3]{1,0:T(1,128)S(1)}, s32[1,3]{1,0:T(1,128)S(1)}, u32[]{:S(2)}, u32[]{:S(2)}) collective-permute-start(s32[1,3]{1,0:T(1,128)S(1)} %copy-done.4), channel_id=1, source_target_pairs={{0,16},{16,32},{32,48},{48,0},{1,17},{17,33},{33,49},{49,1},{2,18}... | collective-permute-start | bytes 44 | tf_op jit(solution)/shard_map/ppermute | solution.py:267
  30.4 2.5 %collective-permute-start.1 = (s32[1,3]{1,0:T(1,128)S(1)}, s32[1,3]{1,0:T(1,128)S(1)}, u32[]{:S(2)}, u32[]{:S(2)}) collective-permute-start(s32[1,3]{1,0:T(1,128)S(1)} %copy-done.4), channel_id=1, source_target_pairs={{0,32},{16,48},{32,0},{48,16},{1,33},{17,49},{33,1},{49,17},{2,34}... | collective-permute-start | bytes 44 | tf_op jit(solution)/shard_map/ppermute | solution.py:267
  32.9 1.1 %collective-permute-start = (s32[1,3]{1,0:T(1,128)S(1)}, s32[1,3]{1,0:T(1,128)S(1)}, u32[]{:S(2)}, u32[]{:S(2)}) collective-permute-start(s32[1,3]{1,0:T(1,128)S(1)} %copy-done.4), channel_id=1, source_target_pairs={{0,48},{16,0},{32,16},{48,32},{1,49},{17,1},{33,17},{49,33},{2,50}... | collective-permute-start | bytes 44 | tf_op jit(solution)/shard_map/ppermute | solution.py:267
  34.5 2.7 %collective-permute-start.6 = (f32[2,4,8,128]{3,2,1,0:T(8,128)S(1)}, f32[2,4,8,128]{3,2,1,0:T(8,128)S(1)}, u32[]{:S(2)}, u32[]{:S(2)}) collective-permute-start(f32[2,4,8,128]{3,2,1,0:T(8,128)S(1)} %get-tuple-element.44), channel_id=1, source_target_pairs={{0,3},{1,2},{2,1},{3,0},{4,7},{5,6},{6,5},{7,4},{8,11},{9,10},{10,... | collective-permute-start | bytes 98312 | tf_op jit(solution)/shard_map/ppermute | solution.py:228
  37.2 3.2 %collective-permute-start.7 = (f32[2,4,8,128]{3,2,1,0:T(8,128)S(1)}, f32[2,4,8,128]{3,2,1,0:T(8,128)S(1)}, u32[]{:S(2)}, u32[]{:S(2)}) collective-permute-start(f32[2,4,8,128]{3,2,1,0:T(8,128)S(1)} %get-tuple-element.45), channel_id=1, source_target_pairs={{0,4},{1,5},{2,6},{3,7},{4,0},{5,1},{6,2},{7,3},{8,12},{9,13},{10,... | collective-permute-start | bytes 98312 | tf_op jit(solution)/shard_map/ppermute | solution.py:228
  41.1 2.4 %collective-permute-start.9 = (f32[2,4,8,128]{3,2,1,0:T(8,128)S(1)}, f32[2,4,8,128]{3,2,1,0:T(8,128)S(1)}, u32[]{:S(2)}, u32[]{:S(2)}) collective-permute-start(f32[2,4,8,128]{3,2,1,0:T(8,128)S(1)} %get-tuple-element.47), channel_id=1, source_target_pairs={{0,6},{1,7},{2,4},{3,5},{4,2},{5,3},{6,0},{7,1},{8,14},{9,15},{10,... | collective-permute-start | bytes 98312 | tf_op jit(solution)/shard_map/ppermute | solution.py:228
  43.9 1.7 %collective-permute-done.8.refs_5_ = f32[2,4,8,128]{3,2,1,0:T(8,128)S(1)} collective-permute-done((f32[2,4,8,128]{3,2,1,0:T(8,128)S(1)}, f32[2,4,8,128]{3,2,1,0:T(8,128)S(1)}, u32[]{:S(2)}, u32[]{:S(2)}) %collective-permute-start.8) | collective-permute-done | bytes 32800 | tf_op jit(solution)/shard_map/ppermute | solution.py:228
  46.4 1.7 %collective-permute-done.10.refs_7_ = f32[2,4,8,128]{3,2,1,0:T(8,128)S(1)} collective-permute-done((f32[2,4,8,128]{3,2,1,0:T(8,128)S(1)}, f32[2,4,8,128]{3,2,1,0:T(8,128)S(1)}, u32[]{:S(2)}, u32[]{:S(2)}) %collective-permute-start.10) | collective-permute-done | bytes 32800 | tf_op jit(solution)/shard_map/ppermute | solution.py:228
  48.1 1.8 %shard_map.67 = f32[32,3,4,8,128]{4,3,2,1,0:T(8,128)} custom-call(s32[1]{0:T(128)} %bitcast.6.x_ref, s32[1]{0:T(128)} %bitcast.yc_ref, s32[1,3]{1,0:T(1,128)S(1)} %copy-done.4, s32[1,3]{1,0:T(1,128)S(1)} %collective-permute-done.m1, s32[1,3]{1,0:T(1,128)S(1)} %collective-permute-done.1.m2, s32[1,3]{1,0:T(1,128)S(1)} %collective-permute-done.2.m3, ...), custom_call_target="tpu_custom_call" | custom-call | tf_op jit(solution)/shard_map/pallas_call | solution.py:281
  49.9 4.5 %all-to-all-start.1 = ((f32[32,3,4,8,128]{4,3,2,1,0:T(8,128)}), f32[32,3,4,8,128]{4,3,2,1,0:T(8,128)}, u32[]{:S(2)}, u32[]{:S(2)}) async-start(f32[32,3,4,8,128]{4,3,2,1,0:T(8,128)} %shard_map.67), calls=%async_computation.1 | async-start | bytes 3145728 | tf_op jit(solution)/shard_map/all_to_all | solution.py:210
  54.5 1.0 shard_map.69
  55.5 6.7 %collective-permute-start.11 = (f32[4,8,8,128]{3,2,1,0:T(8,128)S(1)}, f32[4,8,8,128]{3,2,1,0:T(8,128)S(1)}, u32[]{:S(2)}, u32[]{:S(2)}) collective-permute-start(f32[4,8,8,128]{3,2,1,0:T(8,128)S(1)} %get-tuple-element.53), channel_id=1, source_target_pairs={{0,8},{8,0},{1,9},{9,1},{2,10},{10,2},{3,11},{11,3},{4,12},{12,4},... | collective-permute-start | bytes 393224 | tf_op jit(solution)/shard_map/ppermute | solution.py:298
  62.2 3.7 %collective-permute-done.11.b_ref = f32[4,8,8,128]{3,2,1,0:T(8,128)S(1)} collective-permute-done((f32[4,8,8,128]{3,2,1,0:T(8,128)S(1)}, f32[4,8,8,128]{3,2,1,0:T(8,128)S(1)}, u32[]{:S(2)}, u32[]{:S(2)}) %collective-permute-start.11) | collective-permute-done | bytes 131104 | tf_op jit(solution)/shard_map/ppermute | solution.py:298
  66.0 2.1 %collective-permute-start.12 = (f32[8,8,128]{2,1,0:T(8,128)S(1)}, f32[8,8,128]{2,1,0:T(8,128)S(1)}, u32[]{:S(2)}, u32[]{:S(2)}) collective-permute-start(f32[8,8,128]{2,1,0:T(8,128)S(1)} %get-tuple-element.55), channel_id=1, source_target_pairs={{0,64},{64,0},{128,192},{192,128},{1,65},{65,1},{129,193},{193,129... | collective-permute-start | bytes 98312 | tf_op jit(solution)/shard_map/ppermute | solution.py:228
  68.0 3.5 %collective-permute-start.13 = (f32[8,8,128]{2,1,0:T(8,128)S(1)}, f32[8,8,128]{2,1,0:T(8,128)S(1)}, u32[]{:S(2)}, u32[]{:S(2)}) collective-permute-start(f32[8,8,128]{2,1,0:T(8,128)S(1)} %get-tuple-element.56), channel_id=1, source_target_pairs={{0,128},{64,192},{128,0},{192,64},{1,129},{65,193},{129,1},{193,65... | collective-permute-start | bytes 98312 | tf_op jit(solution)/shard_map/ppermute | solution.py:228
  71.5 0.9 collective-permute-start.14
  73.2 3.0 %collective-permute-done.14.d_ref = f32[8,8,128]{2,1,0:T(8,128)S(1)} collective-permute-done((f32[8,8,128]{2,1,0:T(8,128)S(1)}, f32[8,8,128]{2,1,0:T(8,128)S(1)}, u32[]{:S(2)}, u32[]{:S(2)}) %collective-permute-start.14) | collective-permute-done | bytes 32800 | tf_op jit(solution)/shard_map/ppermute | solution.py:228
  77.0 6.2 %shard_map.68 = f32[16,64,128]{2,1,0:T(8,128)} custom-call(s32[128]{0:T(128)S(1)} %bitcast.15, s32[128]{0:T(128)S(1)} %bitcast.17, s32[1]{0:T(128)} %bitcast.10.count, f32[128,128,128]{2,1,0:T(8,128)} %bitcast.19, f32[64,2048]{1,0:T(8,128)S(1)} %bitcast.13, f32[32,3,4,8,128]{4,3,2,1,0:T(8,128)} %all-to-all-done.1.far_ref, f32[16,64,128]{2,1,0:T(8,128)S(1)} %copy-done.1), custom_call_target="tpu_custom_call" | custom-call | flops 805306368 | bytes 8388608 | tf_op jit(solution)/shard_map/pallas_call | solution.py:302
  83.2 10.0 %all-to-all-start.2 = ((f32[16,64,128]{2,1,0:T(8,128)}), f32[16,64,128]{2,1,0:T(8,128)S(1)}, u32[]{:S(2)}, u32[]{:S(2)}) async-start(f32[16,64,128]{2,1,0:T(8,128)} %shard_map.68), calls=%async_computation.2 | async-start | bytes 1048576 | tf_op jit(solution)/shard_map/all_to_all | solution.py:210
  93.3 1.4 %collective-permute-start.16 = (f32[8,128]{1,0:T(8,128)S(1)}, f32[8,128]{1,0:T(8,128)S(1)}, u32[]{:S(2)}, u32[]{:S(2)}) collective-permute-start(f32[8,128]{1,0:T(8,128)S(1)} %get-tuple-element.69), channel_id=1, source_target_pairs={{0,2},{1,3},{2,0},{3,1},{4,6},{5,7},{6,4},{7,5},{8,10},{9,11},{10,... | collective-permute-start | bytes 12296 | tf_op jit(solution)/shard_map/ppermute | solution.py:228
  95.4 1.6 %collective-permute-start.18 = (f32[8,128]{1,0:T(8,128)S(1)}, f32[8,128]{1,0:T(8,128)S(1)}, u32[]{:S(2)}, u32[]{:S(2)}) collective-permute-start(f32[8,128]{1,0:T(8,128)S(1)} %get-tuple-element.71), channel_id=1, source_target_pairs={{0,4},{1,5},{2,6},{3,7},{4,0},{5,1},{6,2},{7,3},{8,12},{9,13},{10,... | collective-permute-start | bytes 12296 | tf_op jit(solution)/shard_map/ppermute | solution.py:228
  97.1 1.3 %collective-permute-start.19 = (f32[8,128]{1,0:T(8,128)S(1)}, f32[8,128]{1,0:T(8,128)S(1)}, u32[]{:S(2)}, u32[]{:S(2)}) collective-permute-start(f32[8,128]{1,0:T(8,128)S(1)} %get-tuple-element.72), channel_id=1, source_target_pairs={{0,5},{1,4},{2,7},{3,6},{4,1},{5,0},{6,3},{7,2},{8,13},{9,12},{10,... | collective-permute-start | bytes 12296 | tf_op jit(solution)/shard_map/ppermute | solution.py:228
  98.4 2.4 %collective-permute-start.20 = (f32[8,128]{1,0:T(8,128)S(1)}, f32[8,128]{1,0:T(8,128)S(1)}, u32[]{:S(2)}, u32[]{:S(2)}) collective-permute-start(f32[8,128]{1,0:T(8,128)S(1)} %get-tuple-element.73), channel_id=1, source_target_pairs={{0,6},{1,7},{2,4},{3,5},{4,2},{5,3},{6,0},{7,1},{8,14},{9,15},{10,... | collective-permute-start | bytes 12296 | tf_op jit(solution)/shard_map/ppermute | solution.py:228
  100.7 0.9 collective-permute-start.21
  102.4 2.6 %collective-permute-done.21.refs_7_ = f32[8,128]{1,0:T(8,128)S(1)} collective-permute-done((f32[8,128]{1,0:T(8,128)S(1)}, f32[8,128]{1,0:T(8,128)S(1)}, u32[]{:S(2)}, u32[]{:S(2)}) %collective-permute-start.21) | collective-permute-done | bytes 4128 | tf_op jit(solution)/shard_map/ppermute | solution.py:228
  105.0 3.0 %all-to-all-done.2.rows_ref = f32[16,64,128]{2,1,0:T(8,128)S(1)} async-done(((f32[16,64,128]{2,1,0:T(8,128)}), f32[16,64,128]{2,1,0:T(8,128)S(1)}, u32[]{:S(2)}, u32[]{:S(2)}) %all-to-all-start.2) | async-done | bytes 524320 | tf_op jit(solution)/shard_map/all_to_all | solution.py:210
  (37 shorter events, 6.3 us)
Async XLA Ops:
  6.9 9.5 %copy-start = (f32[1,64,2048]{2,1,0:T(8,128)S(1)}, f32[1,64,2048]{2,1,0:T(8,128)}, u32[]{:S(2)}) copy-start(f32[1,64,2048]{2,1,0:T(8,128)} %param.6) | copy-start | bytes 1572868
  6.9 22.3 %copy-start.4 = (s32[1,3]{1,0:T(1,128)S(1)}, s32[1,3]{1,0:T(1,128)}, u32[]{:S(2)}) copy-start(s32[1,3]{1,0:T(1,128)} %m0.3) | copy-start | bytes 40
  6.9 43.0 %all-to-all-start = ((f32[32,3,4,8,128]{4,3,2,1,0:T(8,128)}), f32[32,3,4,8,128]{4,3,2,1,0:T(8,128)S(1)}, u32[]{:S(2)}, u32[]{:S(2)}) async-start(f32[32,3,4,8,128]{4,3,2,1,0:T(8,128)} %get-tuple-element.40), calls=%async_computation | async-start | bytes 3145728 | tf_op jit(solution)/shard_map/all_to_all | solution.py:210
  16.5 10.4 %collective-permute-start.3 = (f32[8,4,8,128]{3,2,1,0:T(8,128)S(1)}, f32[8,4,8,128]{3,2,1,0:T(8,128)S(1)}, u32[]{:S(2)}, u32[]{:S(2)}) collective-permute-start(f32[8,4,8,128]{3,2,1,0:T(8,128)S(1)} %shard_map.65.near_ref), channel_id=1, source_target_pairs={{0,8},{8,0},{1,9},{9,1},{2,10},{10,2},{3,11},{11,3},{4,12},{12,4},... | collective-permute-start | bytes 393224 | tf_op jit(solution)/shard_map/ppermute | solution.py:265
  26.9 14.2 %collective-permute-start.4 = (f32[2,4,8,128]{3,2,1,0:T(8,128)S(1)}, f32[2,4,8,128]{3,2,1,0:T(8,128)S(1)}, u32[]{:S(2)}, u32[]{:S(2)}) collective-permute-start(f32[2,4,8,128]{3,2,1,0:T(8,128)S(1)} %get-tuple-element.42), channel_id=1, source_target_pairs={{0,1},{1,0},{2,3},{3,2},{4,5},{5,4},{6,7},{7,6},{8,9},{9,8},{10,11... | collective-permute-start | bytes 98312 | tf_op jit(solution)/shard_map/ppermute | solution.py:228
  27.9 15.7 %collective-permute-start.5 = (f32[2,4,8,128]{3,2,1,0:T(8,128)S(1)}, f32[2,4,8,128]{3,2,1,0:T(8,128)S(1)}, u32[]{:S(2)}, u32[]{:S(2)}) collective-permute-start(f32[2,4,8,128]{3,2,1,0:T(8,128)S(1)} %get-tuple-element.43), channel_id=1, source_target_pairs={{0,2},{1,3},{2,0},{3,1},{4,6},{5,7},{6,4},{7,5},{8,10},{9,11},{10,... | collective-permute-start | bytes 98312 | tf_op jit(solution)/shard_map/ppermute | solution.py:228
  29.2 5.3 %collective-permute-start.2 = (s32[1,3]{1,0:T(1,128)S(1)}, s32[1,3]{1,0:T(1,128)S(1)}, u32[]{:S(2)}, u32[]{:S(2)}) collective-permute-start(s32[1,3]{1,0:T(1,128)S(1)} %copy-done.4), channel_id=1, source_target_pairs={{0,16},{16,32},{32,48},{48,0},{1,17},{17,33},{33,49},{49,1},{2,18}... | collective-permute-start | bytes 44 | tf_op jit(solution)/shard_map/ppermute | solution.py:267
  30.4 6.7 %collective-permute-start.1 = (s32[1,3]{1,0:T(1,128)S(1)}, s32[1,3]{1,0:T(1,128)S(1)}, u32[]{:S(2)}, u32[]{:S(2)}) collective-permute-start(s32[1,3]{1,0:T(1,128)S(1)} %copy-done.4), channel_id=1, source_target_pairs={{0,32},{16,48},{32,0},{48,16},{1,33},{17,49},{33,1},{49,17},{2,34}... | collective-permute-start | bytes 44 | tf_op jit(solution)/shard_map/ppermute | solution.py:267
  32.9 7.4 %collective-permute-start = (s32[1,3]{1,0:T(1,128)S(1)}, s32[1,3]{1,0:T(1,128)S(1)}, u32[]{:S(2)}, u32[]{:S(2)}) collective-permute-start(s32[1,3]{1,0:T(1,128)S(1)} %copy-done.4), channel_id=1, source_target_pairs={{0,48},{16,0},{32,16},{48,32},{1,49},{17,1},{33,17},{49,33},{2,50}... | collective-permute-start | bytes 44 | tf_op jit(solution)/shard_map/ppermute | solution.py:267
  34.5 9.3 %collective-permute-start.6 = (f32[2,4,8,128]{3,2,1,0:T(8,128)S(1)}, f32[2,4,8,128]{3,2,1,0:T(8,128)S(1)}, u32[]{:S(2)}, u32[]{:S(2)}) collective-permute-start(f32[2,4,8,128]{3,2,1,0:T(8,128)S(1)} %get-tuple-element.44), channel_id=1, source_target_pairs={{0,3},{1,2},{2,1},{3,0},{4,7},{5,6},{6,5},{7,4},{8,11},{9,10},{10,... | collective-permute-start | bytes 98312 | tf_op jit(solution)/shard_map/ppermute | solution.py:228
  37.2 6.7 %collective-permute-start.7 = (f32[2,4,8,128]{3,2,1,0:T(8,128)S(1)}, f32[2,4,8,128]{3,2,1,0:T(8,128)S(1)}, u32[]{:S(2)}, u32[]{:S(2)}) collective-permute-start(f32[2,4,8,128]{3,2,1,0:T(8,128)S(1)} %get-tuple-element.45), channel_id=1, source_target_pairs={{0,4},{1,5},{2,6},{3,7},{4,0},{5,1},{6,2},{7,3},{8,12},{9,13},{10,... | collective-permute-start | bytes 98312 | tf_op jit(solution)/shard_map/ppermute | solution.py:228
  40.3 5.3 %collective-permute-start.8 = (f32[2,4,8,128]{3,2,1,0:T(8,128)S(1)}, f32[2,4,8,128]{3,2,1,0:T(8,128)S(1)}, u32[]{:S(2)}, u32[]{:S(2)}) collective-permute-start(f32[2,4,8,128]{3,2,1,0:T(8,128)S(1)} %get-tuple-element.46), channel_id=1, source_target_pairs={{0,5},{1,4},{2,7},{3,6},{4,1},{5,0},{6,3},{7,2},{8,13},{9,12},{10,... | collective-permute-start | bytes 98312 | tf_op jit(solution)/shard_map/ppermute | solution.py:228
  41.1 5.3 %collective-permute-start.9 = (f32[2,4,8,128]{3,2,1,0:T(8,128)S(1)}, f32[2,4,8,128]{3,2,1,0:T(8,128)S(1)}, u32[]{:S(2)}, u32[]{:S(2)}) collective-permute-start(f32[2,4,8,128]{3,2,1,0:T(8,128)S(1)} %get-tuple-element.47), channel_id=1, source_target_pairs={{0,6},{1,7},{2,4},{3,5},{4,2},{5,3},{6,0},{7,1},{8,14},{9,15},{10,... | collective-permute-start | bytes 98312 | tf_op jit(solution)/shard_map/ppermute | solution.py:228
  43.5 4.6 %collective-permute-start.10 = (f32[2,4,8,128]{3,2,1,0:T(8,128)S(1)}, f32[2,4,8,128]{3,2,1,0:T(8,128)S(1)}, u32[]{:S(2)}, u32[]{:S(2)}) collective-permute-start(f32[2,4,8,128]{3,2,1,0:T(8,128)S(1)} %get-tuple-element.48), channel_id=1, source_target_pairs={{0,7},{1,6},{2,5},{3,4},{4,3},{5,2},{6,1},{7,0},{8,15},{9,14},{10,... | collective-permute-start | bytes 98312 | tf_op jit(solution)/shard_map/ppermute | solution.py:228
  49.9 27.1 %all-to-all-start.1 = ((f32[32,3,4,8,128]{4,3,2,1,0:T(8,128)}), f32[32,3,4,8,128]{4,3,2,1,0:T(8,128)}, u32[]{:S(2)}, u32[]{:S(2)}) async-start(f32[32,3,4,8,128]{4,3,2,1,0:T(8,128)} %shard_map.67), calls=%async_computation.1 | async-start | bytes 3145728 | tf_op jit(solution)/shard_map/all_to_all | solution.py:210
  54.4 22.6 %copy-start.1 = (f32[16,64,128]{2,1,0:T(8,128)S(1)}, f32[16,64,128]{2,1,0:T(8,128)}, u32[]{:S(2)}) copy-start(f32[16,64,128]{2,1,0:T(8,128)} %get-tuple-element.50.self_ref) | copy-start | bytes 1572868
  54.4 22.6 %copy-start.2 = (s32[1,1,128]{2,1,0:T(1,128)S(1)}, s32[1,1,128]{2,1,0:T(1,128)}, u32[]{:S(2)}) copy-start(s32[1,1,128]{2,1,0:T(1,128)} %param.8) | copy-start | bytes 1540
  54.5 22.5 %copy-start.3 = (s32[1,1,128]{2,1,0:T(1,128)S(1)}, s32[1,1,128]{2,1,0:T(1,128)}, u32[]{:S(2)}) copy-start(s32[1,1,128]{2,1,0:T(1,128)} %param.9) | copy-start | bytes 1540
  55.5 10.4 %collective-permute-start.11 = (f32[4,8,8,128]{3,2,1,0:T(8,128)S(1)}, f32[4,8,8,128]{3,2,1,0:T(8,128)S(1)}, u32[]{:S(2)}, u32[]{:S(2)}) collective-permute-start(f32[4,8,8,128]{3,2,1,0:T(8,128)S(1)} %get-tuple-element.53), channel_id=1, source_target_pairs={{0,8},{8,0},{1,9},{9,1},{2,10},{10,2},{3,11},{11,3},{4,12},{12,4},... | collective-permute-start | bytes 393224 | tf_op jit(solution)/shard_map/ppermute | solution.py:298
  66.0 6.4 %collective-permute-start.12 = (f32[8,8,128]{2,1,0:T(8,128)S(1)}, f32[8,8,128]{2,1,0:T(8,128)S(1)}, u32[]{:S(2)}, u32[]{:S(2)}) collective-permute-start(f32[8,8,128]{2,1,0:T(8,128)S(1)} %get-tuple-element.55), channel_id=1, source_target_pairs={{0,64},{64,0},{128,192},{192,128},{1,65},{65,1},{129,193},{193,129... | collective-permute-start | bytes 98312 | tf_op jit(solution)/shard_map/ppermute | solution.py:228
  68.0 5.2 %collective-permute-start.13 = (f32[8,8,128]{2,1,0:T(8,128)S(1)}, f32[8,8,128]{2,1,0:T(8,128)S(1)}, u32[]{:S(2)}, u32[]{:S(2)}) collective-permute-start(f32[8,8,128]{2,1,0:T(8,128)S(1)} %get-tuple-element.56), channel_id=1, source_target_pairs={{0,128},{64,192},{128,0},{192,64},{1,129},{65,193},{129,1},{193,65... | collective-permute-start | bytes 98312 | tf_op jit(solution)/shard_map/ppermute | solution.py:228
  71.5 4.7 %collective-permute-start.14 = (f32[8,8,128]{2,1,0:T(8,128)S(1)}, f32[8,8,128]{2,1,0:T(8,128)S(1)}, u32[]{:S(2)}, u32[]{:S(2)}) collective-permute-start(f32[8,8,128]{2,1,0:T(8,128)S(1)} %get-tuple-element.57), channel_id=1, source_target_pairs={{0,192},{64,128},{128,64},{192,0},{1,193},{65,129},{129,65},{193,1... | collective-permute-start | bytes 98312 | tf_op jit(solution)/shard_map/ppermute | solution.py:228
  83.2 24.8 %all-to-all-start.2 = ((f32[16,64,128]{2,1,0:T(8,128)}), f32[16,64,128]{2,1,0:T(8,128)S(1)}, u32[]{:S(2)}, u32[]{:S(2)}) async-start(f32[16,64,128]{2,1,0:T(8,128)} %shard_map.68), calls=%async_computation.2 | async-start | bytes 1048576 | tf_op jit(solution)/shard_map/all_to_all | solution.py:210
  93.2 5.2 %collective-permute-start.15 = (f32[8,128]{1,0:T(8,128)S(1)}, f32[8,128]{1,0:T(8,128)S(1)}, u32[]{:S(2)}, u32[]{:S(2)}) collective-permute-start(f32[8,128]{1,0:T(8,128)S(1)} %get-tuple-element.68), channel_id=1, source_target_pairs={{0,1},{1,0},{2,3},{3,2},{4,5},{5,4},{6,7},{7,6},{8,9},{9,8},{10,11... | collective-permute-start | bytes 12296 | tf_op jit(solution)/shard_map/ppermute | solution.py:228
  93.3 7.4 %collective-permute-start.16 = (f32[8,128]{1,0:T(8,128)S(1)}, f32[8,128]{1,0:T(8,128)S(1)}, u32[]{:S(2)}, u32[]{:S(2)}) collective-permute-start(f32[8,128]{1,0:T(8,128)S(1)} %get-tuple-element.69), channel_id=1, source_target_pairs={{0,2},{1,3},{2,0},{3,1},{4,6},{5,7},{6,4},{7,5},{8,10},{9,11},{10,... | collective-permute-start | bytes 12296 | tf_op jit(solution)/shard_map/ppermute | solution.py:228
  94.7 6.9 %collective-permute-start.17 = (f32[8,128]{1,0:T(8,128)S(1)}, f32[8,128]{1,0:T(8,128)S(1)}, u32[]{:S(2)}, u32[]{:S(2)}) collective-permute-start(f32[8,128]{1,0:T(8,128)S(1)} %get-tuple-element.70), channel_id=1, source_target_pairs={{0,3},{1,2},{2,1},{3,0},{4,7},{5,6},{6,5},{7,4},{8,11},{9,10},{10,... | collective-permute-start | bytes 12296 | tf_op jit(solution)/shard_map/ppermute | solution.py:228
  95.4 6.2 %collective-permute-start.18 = (f32[8,128]{1,0:T(8,128)S(1)}, f32[8,128]{1,0:T(8,128)S(1)}, u32[]{:S(2)}, u32[]{:S(2)}) collective-permute-start(f32[8,128]{1,0:T(8,128)S(1)} %get-tuple-element.71), channel_id=1, source_target_pairs={{0,4},{1,5},{2,6},{3,7},{4,0},{5,1},{6,2},{7,3},{8,12},{9,13},{10,... | collective-permute-start | bytes 12296 | tf_op jit(solution)/shard_map/ppermute | solution.py:228
  97.1 4.8 %collective-permute-start.19 = (f32[8,128]{1,0:T(8,128)S(1)}, f32[8,128]{1,0:T(8,128)S(1)}, u32[]{:S(2)}, u32[]{:S(2)}) collective-permute-start(f32[8,128]{1,0:T(8,128)S(1)} %get-tuple-element.72), channel_id=1, source_target_pairs={{0,5},{1,4},{2,7},{3,6},{4,1},{5,0},{6,3},{7,2},{8,13},{9,12},{10,... | collective-permute-start | bytes 12296 | tf_op jit(solution)/shard_map/ppermute | solution.py:228
  98.4 4.0 %collective-permute-start.20 = (f32[8,128]{1,0:T(8,128)S(1)}, f32[8,128]{1,0:T(8,128)S(1)}, u32[]{:S(2)}, u32[]{:S(2)}) collective-permute-start(f32[8,128]{1,0:T(8,128)S(1)} %get-tuple-element.73), channel_id=1, source_target_pairs={{0,6},{1,7},{2,4},{3,5},{4,2},{5,3},{6,0},{7,1},{8,14},{9,15},{10,... | collective-permute-start | bytes 12296 | tf_op jit(solution)/shard_map/ppermute | solution.py:228
  100.7 4.2 %collective-permute-start.21 = (f32[8,128]{1,0:T(8,128)S(1)}, f32[8,128]{1,0:T(8,128)S(1)}, u32[]{:S(2)}, u32[]{:S(2)}) collective-permute-start(f32[8,128]{1,0:T(8,128)S(1)} %get-tuple-element.74), channel_id=1, source_target_pairs={{0,7},{1,6},{2,5},{3,4},{4,3},{5,2},{6,1},{7,0},{8,15},{9,14},{10,... | collective-permute-start | bytes 12296 | tf_op jit(solution)/shard_map/ppermute | solution.py:228
where the time goes:
time: 109 us
  starting transfers between devices  68.7 us (63%)
  waiting for transfers between devices  23.1 us (21%)
  Pallas kernels  16.1 us (15%)
    ppermute x17, starting transfers between devices, swaps(): lax.ppermute(arrays[step], axes, [(i, i ^ step) for i in range(count)])  26.6 us
    all_to_all x3, starting transfers between devices, exchange(): return lax.all_to_all(value, axes, 0, 0, tiled=False)  23.9 us
    ppermute x17, waiting for transfers between devices, swaps(): lax.ppermute(arrays[step], axes, [(i, i ^ step) for i in range(count)])  11.4 us
    ppermute x1, starting transfers between devices, on_device(): other = lax.ppermute(near, 'zhi', [(0, 1), (1, 0)])  6.73 us
    ppermute x1, starting transfers between devices, on_device(): other = lax.ppermute(other, 'zhi', [(0, 1), (1, 0)])  6.73 us
    pallas_call x1, Pallas kernels, on_device(): local(columns_kernel, [(FAN, REGIONS - 1, *piece), (blocks, vecs, LANE)],...  6.24 us
    pallas_call x1, Pallas kernels, on_device(): local(rows_kernel, [(blocks, vecs, LANE)], [SMEM] * 3 + [HBM, VMEM, VMEM,...  6.17 us
    ppermute x3, starting transfers between devices, on_device(): lax.ppermute(matchings, 'x', [(i, (i - step) % X) for i in range(X)])  4.77 us
  transfers between devices with their start and end apart: 25, of which 13 were waited for; matrix products, arithmetic and copies ran while one was open for 0% of the time, Pallas kernels for 3%

commit v1 on v0

--- a/solution.py
+++ b/solution.py
@@ -18,8 +18,8 @@
 REGIONS = 4
 SUB = 8
 LANE = 128
-CHUNK = 16
-GROUP = 8
+CHUNK = 32
+GROUPS = (32, 8, 1)
 SMALL = 8 << 20
 LARGE = 56 << 20
 ROWS = 52 << 20
@@ -37,11 +37,24 @@
     return high, (value - high.astype(jnp.float32)).astype(jnp.bfloat16)
 
 
-def product(pair, high, low, dims):
-    both = jnp.concatenate([high, low], axis=1 if dims is BY_COLS else 0)
-    wide = lax.dot_general(pair, both, dims, preferred_element_type=jnp.float32)
+def dot(left, right, dims):
+    return lax.dot_general(left, right, dims, preferred_element_type=jnp.float32)
+
+
+def by_columns(pair, high, low):
     count = pair.shape[0] // 2
+    wide = dot(pair, jnp.concatenate([high, low], axis=1), BY_COLS)
     return wide[:count, :LANE] + wide[count:, :LANE] + wide[:count, LANE:]
+
+
+def by_rows(pair, high, low):
+    count = pair.shape[0] // 2
+    top = jnp.concatenate([pair[:count], pair[:count]], axis=1)
+    bottom = jnp.concatenate([pair[count:], jnp.zeros_like(pair[count:])], axis=1)
+    tall = dot(
+        jnp.concatenate([top, bottom], axis=0), jnp.concatenate([high, low], axis=1), BY_ROWS
+    )
+    return tall[:count] + tall[count:]
 
 
 def pieces_kernel(x_ref, yc_ref, own_ref, out_ref, held, sems):
@@ -138,33 +151,32 @@
 def each_group(copies, live, group):
     for i, copy in enumerate(copies):
         copy.wait()
+        done = 0
         here = jnp.clip(live - i * CHUNK, 0, CHUNK)
-        full = here // GROUP
-
-        def several(step, carry, i=i):
-            group(i * CHUNK + step * GROUP, GROUP)
-            return carry
-
-        def single(step, carry, i=i):
-            group(i * CHUNK + step, 1)
-            return carry
-
-        lax.fori_loop(0, full, several, 0)
-        lax.fori_loop(full * GROUP, here, single, 0)
-
-
-def columns_kernel(rows, cols, count, tiles, own_ref, out_ref, self_ref, held, table, sums, sems):
+        for size in GROUPS:
+
+            def step(at, carry, i=i, size=size):
+                group(i * CHUNK + at * size, size)
+                return carry
+
+            lax.fori_loop(done // size, here // size, step, 0)
+            done = here // size * size
+
+
+def columns_kernel(rows, cols, count, tiles, own, out_ref, self_ref, held, table, sums, near, sems):
+    first = pltpu.make_async_copy(own, near, sems.at[sems.shape[0] - 1])
+    first.start()
     copies = fetch(tiles, held, sems)
     sums[...] = jnp.zeros_like(sums)
-    vecs = own_ref.shape[0]
-    blocks = own_ref.shape[1] // LANE
-    load_table(table, 0, blocks, lambda b: own_ref[:, b * LANE : (b + 1) * LANE], vecs)
+    vecs = near.shape[0]
+    blocks = near.shape[1] // LANE
+    first.wait()
+    load_table(table, 0, blocks, lambda b: near[:, b * LANE : (b + 1) * LANE], vecs)
 
     def group(first, size):
         done = []
         for k in range(size):
-            high, low = halves(held[first + k])
-            done.append(product(table[rows[first + k]], high, low, BY_COLS))
+            done.append(by_columns(table[rows[first + k]], *halves(held[first + k])))
         for k in range(size):
             col = cols[first + k]
             sums[col] += done[k]
@@ -179,26 +191,36 @@
                 out_ref[x * YC + part, slot, zlo] = value[part * SUB : (part + 1) * SUB]
 
 
-def rows_kernel(rows, cols, count, tiles, own_ref, far_ref, self_ref, sums, held, table, sems):
+def rows_kernel(
+    rows, cols, count, tiles, own, far, mine, sums, held, table, near, away, sems
+):
+    last = sems.shape[0] - 3
+    operands = [
+        pltpu.make_async_copy(source, target, sems.at[last + i])
+        for i, (source, target) in enumerate(((own, near), (far, away), (mine, sums)))
+    ]
+    for copy in operands:
+        copy.start()
     copies = fetch(tiles, held, sems)
-    sums[...] = self_ref[...]
-    vecs = own_ref.shape[0]
-    blocks = own_ref.shape[1] // LANE
-    load_table(table, 0, blocks, lambda b: own_ref[:, b * LANE : (b + 1) * LANE], vecs)
+    vecs = near.shape[0]
+    blocks = near.shape[1] // LANE
+    operands[0].wait()
+    load_table(table, 0, blocks, lambda b: near[:, b * LANE : (b + 1) * LANE], vecs)
+    operands[1].wait()
     for slot in range(REGIONS - 1):
 
-        def far(b, slot=slot):
+        def piece(b, slot=slot):
             return jnp.concatenate(
-                [far_ref[b % X * YC + part, slot, b // X] for part in range(YC)], axis=0
+                [away[b % X * YC + part, slot, b // X] for part in range(YC)], axis=0
             )
 
-        load_table(table, (slot + 1) * blocks, blocks, far, vecs)
+        load_table(table, (slot + 1) * blocks, blocks, piece, vecs)
+    operands[2].wait()
 
     def group(first, size):
         done = []
         for k in range(size):
-            high, low = halves(held[first + k])
-            done.append(product(table[cols[first + k]], high, low, BY_ROWS))
+            done.append(by_rows(table[cols[first + k]], *halves(held[first + k])))
         for k in range(size):
             row = rows[first + k]
             sums[row] += done[k]
@@ -245,13 +267,12 @@
         flops=slots * 6 * vecs * LANE * LANE, bytes_accessed=tile_set.size * 4, transcendentals=0
     )
 
-    def tile_scratch(operand, result):
-        sums = [pltpu.VMEM((result, vecs, LANE), jnp.float32)] if result else []
+    def tile_scratch(operand, extra, copies):
         return [
             pltpu.VMEM(tile_set.shape, jnp.float32),
             pltpu.VMEM((operand, 2 * vecs, LANE), jnp.bfloat16),
-            *sums,
-            pltpu.SemaphoreType.DMA((slots // CHUNK,)),
+            *(pltpu.VMEM(shape, jnp.float32) for shape in extra),
+            pltpu.SemaphoreType.DMA((slots // CHUNK + copies,)),
         ]
 
     whole = (YC, *piece)
@@ -270,8 +291,8 @@
     parts, mine = local(
         columns_kernel,
         [(FAN, REGIONS - 1, *piece), (blocks, vecs, LANE)],
-        [SMEM] * 3 + [HBM, VMEM],
-        tile_scratch(blocks, REGIONS * blocks),
+        [SMEM] * 3 + [HBM] * 2,
+        tile_scratch(blocks, [(REGIONS * blocks, vecs, LANE), own.shape], 1),
         LARGE,
         half,
     )(*ids, tile_set, own)
@@ -302,8 +323,8 @@
     (rows,) = local(
         rows_kernel,
         [(blocks, vecs, LANE)],
-        [SMEM] * 3 + [HBM, VMEM, VMEM, VMEM],
-        tile_scratch(REGIONS * blocks, None),
+        [SMEM] * 3 + [HBM] * 4,
+        tile_scratch(REGIONS * blocks, [own.shape, wanted.shape], 3),
         ROWS,
         half,
     )(*ids, tile_set, own, far, mine)

time: 109 us -> 105 us (0.963)
  starting transfers between devices: 68.7 us -> 66.9 us
  Pallas kernels: 16.1 us -> 14.8 us
    all_to_all x3, starting transfers between devices: 23.9 us -> 21.4 us  [exchange(): return lax.all_to_all(value, axes, 0, 0, tiled=False)]
where the time goes in v1:
time: 105 us
  starting transfers between devices  66.9 us (64%)
  waiting for transfers between devices  22.2 us (21%)
  Pallas kernels  14.8 us (14%)
    ppermute x17, starting transfers between devices, swaps(): lax.ppermute(arrays[step], axes, [(i, i ^ step) for i in range(count)])  26.7 us
    all_to_all x3, starting transfers between devices, exchange(): return lax.all_to_all(value, axes, 0, 0, tiled=False)  21.4 us
    ppermute x17, waiting for transfers between devices, swaps(): lax.ppermute(arrays[step], axes, [(i, i ^ step) for i in range(count)])  11.2 us
    ppermute x1, starting transfers between devices, on_device(): other = lax.ppermute(near, 'zhi', [(0, 1), (1, 0)])  7 us
    ppermute x1, starting transfers between devices, on_device(): other = lax.ppermute(other, 'zhi', [(0, 1), (1, 0)])  7 us
    pallas_call x1, Pallas kernels, on_device(): local(columns_kernel, [(FAN, REGIONS - 1, *piece), (blocks, vecs, LANE)],...  5.77 us
    pallas_call x1, Pallas kernels, on_device(): local(rows_kernel, [(blocks, vecs, LANE)], [SMEM] * 3 + [HBM] * 4, tile_s...  5.36 us
    ppermute x3, starting transfers between devices, on_device(): lax.ppermute(matchings, 'x', [(i, (i - step) % X) for i in range(X)])  4.77 us
  transfers between devices with their start and end apart: 25, of which 13 were waited for; matrix products, arithmetic and copies ran while one was open for 0% of the time, Pallas kernels for 3%

profile of v1, /device:TPU:1, one launch (start us, length us, event | category | flops | bytes accessed | tf_op | source)
XLA Modules:
  0.0 104.7 jit_solution(1267961305837829788)
XLA Ops:
  0.7 5.8 %shard_map.64 = (f32[32,3,4,8,128]{4,3,2,1,0:T(8,128)}, f32[16,64,128]{2,1,0:T(8,128)}) custom-call(s32[128]{0:T(128)} %bitcast.14, s32[128]{0:T(128)} %bitcast.16, s32[1]{0:T(128)} %bitcast.9.count, f32[128,128,128]{2,1,0:T(8,128)} %bitcast.18, f32[64,2048]{1,0:T(8,128)} %bitcast.11), custom_call_target="tpu_custom_call" | custom-call | flops 805306368 | bytes 8388608 | tf_op jit(solution)/shard_map/pallas_call | solution.py:291
  6.5 8.7 %all-to-all-start = ((f32[32,3,4,8,128]{4,3,2,1,0:T(8,128)}), f32[32,3,4,8,128]{4,3,2,1,0:T(8,128)S(1)}, u32[]{:S(2)}, u32[]{:S(2)}) async-start(f32[32,3,4,8,128]{4,3,2,1,0:T(8,128)} %get-tuple-element.40), calls=%async_computation | async-start | bytes 3145728 | tf_op jit(solution)/shard_map/all_to_all | solution.py:232
  15.3 7.0 %collective-permute-start.3 = (f32[8,4,8,128]{3,2,1,0:T(8,128)S(1)}, f32[8,4,8,128]{3,2,1,0:T(8,128)S(1)}, u32[]{:S(2)}, u32[]{:S(2)}) collective-permute-start(f32[8,4,8,128]{3,2,1,0:T(8,128)S(1)} %shard_map.65.near_ref), channel_id=1, source_target_pairs={{0,8},{8,0},{1,9},{9,1},{2,10},{10,2},{3,11},{11,3},{4,12},{12,4},... | collective-permute-start | bytes 393224 | tf_op jit(solution)/shard_map/ppermute | solution.py:286
  22.3 3.6 %collective-permute-done.3.other_ref = f32[8,4,8,128]{3,2,1,0:T(8,128)S(1)} collective-permute-done((f32[8,4,8,128]{3,2,1,0:T(8,128)S(1)}, f32[8,4,8,128]{3,2,1,0:T(8,128)S(1)}, u32[]{:S(2)}, u32[]{:S(2)}) %collective-permute-start.3) | collective-permute-done | bytes 131104 | tf_op jit(solution)/shard_map/ppermute | solution.py:286
  26.0 1.0 collective-permute-start.4
  27.0 1.4 %collective-permute-start.5 = (f32[2,4,8,128]{3,2,1,0:T(8,128)S(1)}, f32[2,4,8,128]{3,2,1,0:T(8,128)S(1)}, u32[]{:S(2)}, u32[]{:S(2)}) collective-permute-start(f32[2,4,8,128]{3,2,1,0:T(8,128)S(1)} %get-tuple-element.43), channel_id=1, source_target_pairs={{0,2},{1,3},{2,0},{3,1},{4,6},{5,7},{6,4},{7,5},{8,10},{9,11},{10,... | collective-permute-start | bytes 98312 | tf_op jit(solution)/shard_map/ppermute | solution.py:250
  28.3 1.2 %collective-permute-start.2 = (s32[1,3]{1,0:T(1,128)S(1)}, s32[1,3]{1,0:T(1,128)S(1)}, u32[]{:S(2)}, u32[]{:S(2)}) collective-permute-start(s32[1,3]{1,0:T(1,128)S(1)} %copy-done.4), channel_id=1, source_target_pairs={{0,16},{16,32},{32,48},{48,0},{1,17},{17,33},{33,49},{49,1},{2,18}... | collective-permute-start | bytes 44 | tf_op jit(solution)/shard_map/ppermute | solution.py:288
  29.5 2.5 %collective-permute-start.1 = (s32[1,3]{1,0:T(1,128)S(1)}, s32[1,3]{1,0:T(1,128)S(1)}, u32[]{:S(2)}, u32[]{:S(2)}) collective-permute-start(s32[1,3]{1,0:T(1,128)S(1)} %copy-done.4), channel_id=1, source_target_pairs={{0,32},{16,48},{32,0},{48,16},{1,33},{17,49},{33,1},{49,17},{2,34}... | collective-permute-start | bytes 44 | tf_op jit(solution)/shard_map/ppermute | solution.py:288
  32.0 1.1 %collective-permute-start = (s32[1,3]{1,0:T(1,128)S(1)}, s32[1,3]{1,0:T(1,128)S(1)}, u32[]{:S(2)}, u32[]{:S(2)}) collective-permute-start(s32[1,3]{1,0:T(1,128)S(1)} %copy-done.4), channel_id=1, source_target_pairs={{0,48},{16,0},{32,16},{48,32},{1,49},{17,1},{33,17},{49,33},{2,50}... | collective-permute-start | bytes 44 | tf_op jit(solution)/shard_map/ppermute | solution.py:288
  33.3 2.7 %collective-permute-start.6 = (f32[2,4,8,128]{3,2,1,0:T(8,128)S(1)}, f32[2,4,8,128]{3,2,1,0:T(8,128)S(1)}, u32[]{:S(2)}, u32[]{:S(2)}) collective-permute-start(f32[2,4,8,128]{3,2,1,0:T(8,128)S(1)} %get-tuple-element.44), channel_id=1, source_target_pairs={{0,3},{1,2},{2,1},{3,0},{4,7},{5,6},{6,5},{7,4},{8,11},{9,10},{10,... | collective-permute-start | bytes 98312 | tf_op jit(solution)/shard_map/ppermute | solution.py:250
  36.0 3.2 %collective-permute-start.7 = (f32[2,4,8,128]{3,2,1,0:T(8,128)S(1)}, f32[2,4,8,128]{3,2,1,0:T(8,128)S(1)}, u32[]{:S(2)}, u32[]{:S(2)}) collective-permute-start(f32[2,4,8,128]{3,2,1,0:T(8,128)S(1)} %get-tuple-element.45), channel_id=1, source_target_pairs={{0,4},{1,5},{2,6},{3,7},{4,0},{5,1},{6,2},{7,3},{8,12},{9,13},{10,... | collective-permute-start | bytes 98312 | tf_op jit(solution)/shard_map/ppermute | solution.py:250
  39.9 2.4 %collective-permute-start.9 = (f32[2,4,8,128]{3,2,1,0:T(8,128)S(1)}, f32[2,4,8,128]{3,2,1,0:T(8,128)S(1)}, u32[]{:S(2)}, u32[]{:S(2)}) collective-permute-start(f32[2,4,8,128]{3,2,1,0:T(8,128)S(1)} %get-tuple-element.47), channel_id=1, source_target_pairs={{0,6},{1,7},{2,4},{3,5},{4,2},{5,3},{6,0},{7,1},{8,14},{9,15},{10,... | collective-permute-start | bytes 98312 | tf_op jit(solution)/shard_map/ppermute | solution.py:250
  42.7 1.7 %collective-permute-done.8.refs_5_ = f32[2,4,8,128]{3,2,1,0:T(8,128)S(1)} collective-permute-done((f32[2,4,8,128]{3,2,1,0:T(8,128)S(1)}, f32[2,4,8,128]{3,2,1,0:T(8,128)S(1)}, u32[]{:S(2)}, u32[]{:S(2)}) %collective-permute-start.8) | collective-permute-done | bytes 32800 | tf_op jit(solution)/shard_map/ppermute | solution.py:250
  45.2 1.7 %collective-permute-done.10.refs_7_ = f32[2,4,8,128]{3,2,1,0:T(8,128)S(1)} collective-permute-done((f32[2,4,8,128]{3,2,1,0:T(8,128)S(1)}, f32[2,4,8,128]{3,2,1,0:T(8,128)S(1)}, u32[]{:S(2)}, u32[]{:S(2)}) %collective-permute-start.10) | collective-permute-done | bytes 32800 | tf_op jit(solution)/shard_map/ppermute | solution.py:250
  46.9 1.8 %shard_map.67 = f32[32,3,4,8,128]{4,3,2,1,0:T(8,128)} custom-call(s32[1]{0:T(128)} %bitcast.6.x_ref, s32[1]{0:T(128)} %bitcast.yc_ref, s32[1,3]{1,0:T(1,128)S(1)} %copy-done.4, s32[1,3]{1,0:T(1,128)S(1)} %collective-permute-done.m1, s32[1,3]{1,0:T(1,128)S(1)} %collective-permute-done.1.m2, s32[1,3]{1,0:T(1,128)S(1)} %collective-permute-done.2.m3, ...), custom_call_target="tpu_custom_call" | custom-call | tf_op jit(solution)/shard_map/pallas_call | solution.py:302
  48.8 4.7 %all-to-all-start.1 = ((f32[32,3,4,8,128]{4,3,2,1,0:T(8,128)}), f32[32,3,4,8,128]{4,3,2,1,0:T(8,128)}, u32[]{:S(2)}, u32[]{:S(2)}) async-start(f32[32,3,4,8,128]{4,3,2,1,0:T(8,128)} %shard_map.67), calls=%async_computation.1 | async-start | bytes 3145728 | tf_op jit(solution)/shard_map/all_to_all | solution.py:232
  53.5 1.0 shard_map.69
  54.5 7.0 %collective-permute-start.11 = (f32[4,8,8,128]{3,2,1,0:T(8,128)S(1)}, f32[4,8,8,128]{3,2,1,0:T(8,128)S(1)}, u32[]{:S(2)}, u32[]{:S(2)}) collective-permute-start(f32[4,8,8,128]{3,2,1,0:T(8,128)S(1)} %get-tuple-element.53), channel_id=1, source_target_pairs={{0,8},{8,0},{1,9},{9,1},{2,10},{10,2},{3,11},{11,3},{4,12},{12,4},... | collective-permute-start | bytes 393224 | tf_op jit(solution)/shard_map/ppermute | solution.py:319
  61.5 3.7 %collective-permute-done.11.b_ref = f32[4,8,8,128]{3,2,1,0:T(8,128)S(1)} collective-permute-done((f32[4,8,8,128]{3,2,1,0:T(8,128)S(1)}, f32[4,8,8,128]{3,2,1,0:T(8,128)S(1)}, u32[]{:S(2)}, u32[]{:S(2)}) %collective-permute-start.11) | collective-permute-done | bytes 131104 | tf_op jit(solution)/shard_map/ppermute | solution.py:319
  65.2 1.2 %collective-permute-start.12 = (f32[8,8,128]{2,1,0:T(8,128)S(1)}, f32[8,8,128]{2,1,0:T(8,128)S(1)}, u32[]{:S(2)}, u32[]{:S(2)}) collective-permute-start(f32[8,8,128]{2,1,0:T(8,128)S(1)} %get-tuple-element.55), channel_id=1, source_target_pairs={{0,64},{64,0},{128,192},{192,128},{1,65},{65,1},{129,193},{193,129... | collective-permute-start | bytes 98312 | tf_op jit(solution)/shard_map/ppermute | solution.py:250
  66.5 4.2 %collective-permute-start.13 = (f32[8,8,128]{2,1,0:T(8,128)S(1)}, f32[8,8,128]{2,1,0:T(8,128)S(1)}, u32[]{:S(2)}, u32[]{:S(2)}) collective-permute-start(f32[8,8,128]{2,1,0:T(8,128)S(1)} %get-tuple-element.56), channel_id=1, source_target_pairs={{0,128},{64,192},{128,0},{192,64},{1,129},{65,193},{129,1},{193,65... | collective-permute-start | bytes 98312 | tf_op jit(solution)/shard_map/ppermute | solution.py:250
  70.7 1.1 %collective-permute-start.14 = (f32[8,8,128]{2,1,0:T(8,128)S(1)}, f32[8,8,128]{2,1,0:T(8,128)S(1)}, u32[]{:S(2)}, u32[]{:S(2)}) collective-permute-start(f32[8,8,128]{2,1,0:T(8,128)S(1)} %get-tuple-element.57), channel_id=1, source_target_pairs={{0,192},{64,128},{128,64},{192,0},{1,193},{65,129},{129,65},{193,1... | collective-permute-start | bytes 98312 | tf_op jit(solution)/shard_map/ppermute | solution.py:250
  72.4 3.0 %collective-permute-done.14.d_ref = f32[8,8,128]{2,1,0:T(8,128)S(1)} collective-permute-done((f32[8,8,128]{2,1,0:T(8,128)S(1)}, f32[8,8,128]{2,1,0:T(8,128)S(1)}, u32[]{:S(2)}, u32[]{:S(2)}) %collective-permute-start.14) | collective-permute-done | bytes 32800 | tf_op jit(solution)/shard_map/ppermute | solution.py:250
  75.8 5.4 %shard_map.68 = f32[16,64,128]{2,1,0:T(8,128)} custom-call(s32[128]{0:T(128)S(1)} %bitcast.15, s32[128]{0:T(128)S(1)} %bitcast.17, s32[1]{0:T(128)} %bitcast.10.count, f32[128,128,128]{2,1,0:T(8,128)} %bitcast.19, f32[64,2048]{1,0:T(8,128)S(1)} %bitcast.13, f32[32,3,4,8,128]{4,3,2,1,0:T(8,128)} %all-to-all-done.1.far, f32[16,64,128]{2,1,0:T(8,128)S(1)} %copy-done.1), custom_call_target="tpu_custom_call" | custom-call | flops 805306368 | bytes 8388608 | tf_op jit(solution)/shard_map/pallas_call | solution.py:323
  81.2 8.0 %all-to-all-start.2 = ((f32[16,64,128]{2,1,0:T(8,128)}), f32[16,64,128]{2,1,0:T(8,128)S(1)}, u32[]{:S(2)}, u32[]{:S(2)}) async-start(f32[16,64,128]{2,1,0:T(8,128)} %shard_map.68), calls=%async_computation.2 | async-start | bytes 1048576 | tf_op jit(solution)/shard_map/all_to_all | solution.py:232
  89.3 1.4 %collective-permute-start.16 = (f32[8,128]{1,0:T(8,128)S(1)}, f32[8,128]{1,0:T(8,128)S(1)}, u32[]{:S(2)}, u32[]{:S(2)}) collective-permute-start(f32[8,128]{1,0:T(8,128)S(1)} %get-tuple-element.69), channel_id=1, source_target_pairs={{0,2},{1,3},{2,0},{3,1},{4,6},{5,7},{6,4},{7,5},{8,10},{9,11},{10,... | collective-permute-start | bytes 12296 | tf_op jit(solution)/shard_map/ppermute | solution.py:250
  91.5 1.7 %collective-permute-start.18 = (f32[8,128]{1,0:T(8,128)S(1)}, f32[8,128]{1,0:T(8,128)S(1)}, u32[]{:S(2)}, u32[]{:S(2)}) collective-permute-start(f32[8,128]{1,0:T(8,128)S(1)} %get-tuple-element.71), channel_id=1, source_target_pairs={{0,4},{1,5},{2,6},{3,7},{4,0},{5,1},{6,2},{7,3},{8,12},{9,13},{10,... | collective-permute-start | bytes 12296 | tf_op jit(solution)/shard_map/ppermute | solution.py:250
  93.1 1.3 %collective-permute-start.19 = (f32[8,128]{1,0:T(8,128)S(1)}, f32[8,128]{1,0:T(8,128)S(1)}, u32[]{:S(2)}, u32[]{:S(2)}) collective-permute-start(f32[8,128]{1,0:T(8,128)S(1)} %get-tuple-element.72), channel_id=1, source_target_pairs={{0,5},{1,4},{2,7},{3,6},{4,1},{5,0},{6,3},{7,2},{8,13},{9,12},{10,... | collective-permute-start | bytes 12296 | tf_op jit(solution)/shard_map/ppermute | solution.py:250
  94.4 2.4 %collective-permute-start.20 = (f32[8,128]{1,0:T(8,128)S(1)}, f32[8,128]{1,0:T(8,128)S(1)}, u32[]{:S(2)}, u32[]{:S(2)}) collective-permute-start(f32[8,128]{1,0:T(8,128)S(1)} %get-tuple-element.73), channel_id=1, source_target_pairs={{0,6},{1,7},{2,4},{3,5},{4,2},{5,3},{6,0},{7,1},{8,14},{9,15},{10,... | collective-permute-start | bytes 12296 | tf_op jit(solution)/shard_map/ppermute | solution.py:250
  96.8 0.9 collective-permute-start.21
  98.4 2.6 %collective-permute-done.21.refs_7_ = f32[8,128]{1,0:T(8,128)S(1)} collective-permute-done((f32[8,128]{1,0:T(8,128)S(1)}, f32[8,128]{1,0:T(8,128)S(1)}, u32[]{:S(2)}, u32[]{:S(2)}) %collective-permute-start.21) | collective-permute-done | bytes 4128 | tf_op jit(solution)/shard_map/ppermute | solution.py:250
  101.0 3.0 %all-to-all-done.2.rows_ref = f32[16,64,128]{2,1,0:T(8,128)S(1)} async-done(((f32[16,64,128]{2,1,0:T(8,128)}), f32[16,64,128]{2,1,0:T(8,128)S(1)}, u32[]{:S(2)}, u32[]{:S(2)}) %all-to-all-start.2) | async-done | bytes 524320 | tf_op jit(solution)/shard_map/all_to_all | solution.py:232
  (37 shorter events, 5.5 us)
Async XLA Ops:
  6.4 8.8 %copy-start = (f32[1,64,2048]{2,1,0:T(8,128)S(1)}, f32[1,64,2048]{2,1,0:T(8,128)}, u32[]{:S(2)}) copy-start(f32[1,64,2048]{2,1,0:T(8,128)} %param.6) | copy-start | bytes 1572868
  6.4 21.9 %copy-start.4 = (s32[1,3]{1,0:T(1,128)S(1)}, s32[1,3]{1,0:T(1,128)}, u32[]{:S(2)}) copy-start(s32[1,3]{1,0:T(1,128)} %m0.3) | copy-start | bytes 40
  6.5 42.3 %all-to-all-start = ((f32[32,3,4,8,128]{4,3,2,1,0:T(8,128)}), f32[32,3,4,8,128]{4,3,2,1,0:T(8,128)S(1)}, u32[]{:S(2)}, u32[]{:S(2)}) async-start(f32[32,3,4,8,128]{4,3,2,1,0:T(8,128)} %get-tuple-element.40), calls=%async_computation | async-start | bytes 3145728 | tf_op jit(solution)/shard_map/all_to_all | solution.py:232
  15.3 10.6 %collective-permute-start.3 = (f32[8,4,8,128]{3,2,1,0:T(8,128)S(1)}, f32[8,4,8,128]{3,2,1,0:T(8,128)S(1)}, u32[]{:S(2)}, u32[]{:S(2)}) collective-permute-start(f32[8,4,8,128]{3,2,1,0:T(8,128)S(1)} %shard_map.65.near_ref), channel_id=1, source_target_pairs={{0,8},{8,0},{1,9},{9,1},{2,10},{10,2},{3,11},{11,3},{4,12},{12,4},... | collective-permute-start | bytes 393224 | tf_op jit(solution)/shard_map/ppermute | solution.py:286
  26.0 14.0 %collective-permute-start.4 = (f32[2,4,8,128]{3,2,1,0:T(8,128)S(1)}, f32[2,4,8,128]{3,2,1,0:T(8,128)S(1)}, u32[]{:S(2)}, u32[]{:S(2)}) collective-permute-start(f32[2,4,8,128]{3,2,1,0:T(8,128)S(1)} %get-tuple-element.42), channel_id=1, source_target_pairs={{0,1},{1,0},{2,3},{3,2},{4,5},{5,4},{6,7},{7,6},{8,9},{9,8},{10,11... | collective-permute-start | bytes 98312 | tf_op jit(solution)/shard_map/ppermute | solution.py:250
  27.0 15.4 %collective-permute-start.5 = (f32[2,4,8,128]{3,2,1,0:T(8,128)S(1)}, f32[2,4,8,128]{3,2,1,0:T(8,128)S(1)}, u32[]{:S(2)}, u32[]{:S(2)}) collective-permute-start(f32[2,4,8,128]{3,2,1,0:T(8,128)S(1)} %get-tuple-element.43), channel_id=1, source_target_pairs={{0,2},{1,3},{2,0},{3,1},{4,6},{5,7},{6,4},{7,5},{8,10},{9,11},{10,... | collective-permute-start | bytes 98312 | tf_op jit(solution)/shard_map/ppermute | solution.py:250
  28.3 5.0 %collective-permute-start.2 = (s32[1,3]{1,0:T(1,128)S(1)}, s32[1,3]{1,0:T(1,128)S(1)}, u32[]{:S(2)}, u32[]{:S(2)}) collective-permute-start(s32[1,3]{1,0:T(1,128)S(1)} %copy-done.4), channel_id=1, source_target_pairs={{0,16},{16,32},{32,48},{48,0},{1,17},{17,33},{33,49},{49,1},{2,18}... | collective-permute-start | bytes 44 | tf_op jit(solution)/shard_map/ppermute | solution.py:288
  29.5 6.5 %collective-permute-start.1 = (s32[1,3]{1,0:T(1,128)S(1)}, s32[1,3]{1,0:T(1,128)S(1)}, u32[]{:S(2)}, u32[]{:S(2)}) collective-permute-start(s32[1,3]{1,0:T(1,128)S(1)} %copy-done.4), channel_id=1, source_target_pairs={{0,32},{16,48},{32,0},{48,16},{1,33},{17,49},{33,1},{49,17},{2,34}... | collective-permute-start | bytes 44 | tf_op jit(solution)/shard_map/ppermute | solution.py:288
  32.0 7.2 %collective-permute-start = (s32[1,3]{1,0:T(1,128)S(1)}, s32[1,3]{1,0:T(1,128)S(1)}, u32[]{:S(2)}, u32[]{:S(2)}) collective-permute-start(s32[1,3]{1,0:T(1,128)S(1)} %copy-done.4), channel_id=1, source_target_pairs={{0,48},{16,0},{32,16},{48,32},{1,49},{17,1},{33,17},{49,33},{2,50}... | collective-permute-start | bytes 44 | tf_op jit(solution)/shard_map/ppermute | solution.py:288
  33.3 9.3 %collective-permute-start.6 = (f32[2,4,8,128]{3,2,1,0:T(8,128)S(1)}, f32[2,4,8,128]{3,2,1,0:T(8,128)S(1)}, u32[]{:S(2)}, u32[]{:S(2)}) collective-permute-start(f32[2,4,8,128]{3,2,1,0:T(8,128)S(1)} %get-tuple-element.44), channel_id=1, source_target_pairs={{0,3},{1,2},{2,1},{3,0},{4,7},{5,6},{6,5},{7,4},{8,11},{9,10},{10,... | collective-permute-start | bytes 98312 | tf_op jit(solution)/shard_map/ppermute | solution.py:250
  36.0 6.7 %collective-permute-start.7 = (f32[2,4,8,128]{3,2,1,0:T(8,128)S(1)}, f32[2,4,8,128]{3,2,1,0:T(8,128)S(1)}, u32[]{:S(2)}, u32[]{:S(2)}) collective-permute-start(f32[2,4,8,128]{3,2,1,0:T(8,128)S(1)} %get-tuple-element.45), channel_id=1, source_target_pairs={{0,4},{1,5},{2,6},{3,7},{4,0},{5,1},{6,2},{7,3},{8,12},{9,13},{10,... | collective-permute-start | bytes 98312 | tf_op jit(solution)/shard_map/ppermute | solution.py:250
  39.1 5.3 %collective-permute-start.8 = (f32[2,4,8,128]{3,2,1,0:T(8,128)S(1)}, f32[2,4,8,128]{3,2,1,0:T(8,128)S(1)}, u32[]{:S(2)}, u32[]{:S(2)}) collective-permute-start(f32[2,4,8,128]{3,2,1,0:T(8,128)S(1)} %get-tuple-element.46), channel_id=1, source_target_pairs={{0,5},{1,4},{2,7},{3,6},{4,1},{5,0},{6,3},{7,2},{8,13},{9,12},{10,... | collective-permute-start | bytes 98312 | tf_op jit(solution)/shard_map/ppermute | solution.py:250
  39.9 5.3 %collective-permute-start.9 = (f32[2,4,8,128]{3,2,1,0:T(8,128)S(1)}, f32[2,4,8,128]{3,2,1,0:T(8,128)S(1)}, u32[]{:S(2)}, u32[]{:S(2)}) collective-permute-start(f32[2,4,8,128]{3,2,1,0:T(8,128)S(1)} %get-tuple-element.47), channel_id=1, source_target_pairs={{0,6},{1,7},{2,4},{3,5},{4,2},{5,3},{6,0},{7,1},{8,14},{9,15},{10,... | collective-permute-start | bytes 98312 | tf_op jit(solution)/shard_map/ppermute | solution.py:250
  42.4 4.6 %collective-permute-start.10 = (f32[2,4,8,128]{3,2,1,0:T(8,128)S(1)}, f32[2,4,8,128]{3,2,1,0:T(8,128)S(1)}, u32[]{:S(2)}, u32[]{:S(2)}) collective-permute-start(f32[2,4,8,128]{3,2,1,0:T(8,128)S(1)} %get-tuple-element.48), channel_id=1, source_target_pairs={{0,7},{1,6},{2,5},{3,4},{4,3},{5,2},{6,1},{7,0},{8,15},{9,14},{10,... | collective-permute-start | bytes 98312 | tf_op jit(solution)/shard_map/ppermute | solution.py:250
  48.8 27.1 %all-to-all-start.1 = ((f32[32,3,4,8,128]{4,3,2,1,0:T(8,128)}), f32[32,3,4,8,128]{4,3,2,1,0:T(8,128)}, u32[]{:S(2)}, u32[]{:S(2)}) async-start(f32[32,3,4,8,128]{4,3,2,1,0:T(8,128)} %shard_map.67), calls=%async_computation.1 | async-start | bytes 3145728 | tf_op jit(solution)/shard_map/all_to_all | solution.py:232
  53.4 22.4 %copy-start.1 = (f32[16,64,128]{2,1,0:T(8,128)S(1)}, f32[16,64,128]{2,1,0:T(8,128)}, u32[]{:S(2)}) copy-start(f32[16,64,128]{2,1,0:T(8,128)} %get-tuple-element.50.mine) | copy-start | bytes 1572868
  53.4 22.4 %copy-start.2 = (s32[1,1,128]{2,1,0:T(1,128)S(1)}, s32[1,1,128]{2,1,0:T(1,128)}, u32[]{:S(2)}) copy-start(s32[1,1,128]{2,1,0:T(1,128)} %param.8) | copy-start | bytes 1540
  53.5 22.4 %copy-start.3 = (s32[1,1,128]{2,1,0:T(1,128)S(1)}, s32[1,1,128]{2,1,0:T(1,128)}, u32[]{:S(2)}) copy-start(s32[1,1,128]{2,1,0:T(1,128)} %param.9) | copy-start | bytes 1540
  54.5 10.7 %collective-permute-start.11 = (f32[4,8,8,128]{3,2,1,0:T(8,128)S(1)}, f32[4,8,8,128]{3,2,1,0:T(8,128)S(1)}, u32[]{:S(2)}, u32[]{:S(2)}) collective-permute-start(f32[4,8,8,128]{3,2,1,0:T(8,128)S(1)} %get-tuple-element.53), channel_id=1, source_target_pairs={{0,8},{8,0},{1,9},{9,1},{2,10},{10,2},{3,11},{11,3},{4,12},{12,4},... | collective-permute-start | bytes 393224 | tf_op jit(solution)/shard_map/ppermute | solution.py:319
  65.2 6.6 %collective-permute-start.12 = (f32[8,8,128]{2,1,0:T(8,128)S(1)}, f32[8,8,128]{2,1,0:T(8,128)S(1)}, u32[]{:S(2)}, u32[]{:S(2)}) collective-permute-start(f32[8,8,128]{2,1,0:T(8,128)S(1)} %get-tuple-element.55), channel_id=1, source_target_pairs={{0,64},{64,0},{128,192},{192,128},{1,65},{65,1},{129,193},{193,129... | collective-permute-start | bytes 98312 | tf_op jit(solution)/shard_map/ppermute | solution.py:250
  66.5 6.0 %collective-permute-start.13 = (f32[8,8,128]{2,1,0:T(8,128)S(1)}, f32[8,8,128]{2,1,0:T(8,128)S(1)}, u32[]{:S(2)}, u32[]{:S(2)}) collective-permute-start(f32[8,8,128]{2,1,0:T(8,128)S(1)} %get-tuple-element.56), channel_id=1, source_target_pairs={{0,128},{64,192},{128,0},{192,64},{1,129},{65,193},{129,1},{193,65... | collective-permute-start | bytes 98312 | tf_op jit(solution)/shard_map/ppermute | solution.py:250
  70.7 4.7 %collective-permute-start.14 = (f32[8,8,128]{2,1,0:T(8,128)S(1)}, f32[8,8,128]{2,1,0:T(8,128)S(1)}, u32[]{:S(2)}, u32[]{:S(2)}) collective-permute-start(f32[8,8,128]{2,1,0:T(8,128)S(1)} %get-tuple-element.57), channel_id=1, source_target_pairs={{0,192},{64,128},{128,64},{192,0},{1,193},{65,129},{129,65},{193,1... | collective-permute-start | bytes 98312 | tf_op jit(solution)/shard_map/ppermute | solution.py:250
  81.2 22.9 %all-to-all-start.2 = ((f32[16,64,128]{2,1,0:T(8,128)}), f32[16,64,128]{2,1,0:T(8,128)S(1)}, u32[]{:S(2)}, u32[]{:S(2)}) async-start(f32[16,64,128]{2,1,0:T(8,128)} %shard_map.68), calls=%async_computation.2 | async-start | bytes 1048576 | tf_op jit(solution)/shard_map/all_to_all | solution.py:232
  89.2 5.2 %collective-permute-start.15 = (f32[8,128]{1,0:T(8,128)S(1)}, f32[8,128]{1,0:T(8,128)S(1)}, u32[]{:S(2)}, u32[]{:S(2)}) collective-permute-start(f32[8,128]{1,0:T(8,128)S(1)} %get-tuple-element.68), channel_id=1, source_target_pairs={{0,1},{1,0},{2,3},{3,2},{4,5},{5,4},{6,7},{7,6},{8,9},{9,8},{10,11... | collective-permute-start | bytes 12296 | tf_op jit(solution)/shard_map/ppermute | solution.py:250
  89.3 7.5 %collective-permute-start.16 = (f32[8,128]{1,0:T(8,128)S(1)}, f32[8,128]{1,0:T(8,128)S(1)}, u32[]{:S(2)}, u32[]{:S(2)}) collective-permute-start(f32[8,128]{1,0:T(8,128)S(1)} %get-tuple-element.69), channel_id=1, source_target_pairs={{0,2},{1,3},{2,0},{3,1},{4,6},{5,7},{6,4},{7,5},{8,10},{9,11},{10,... | collective-permute-start | bytes 12296 | tf_op jit(solution)/shard_map/ppermute | solution.py:250
  90.8 6.9 %collective-permute-start.17 = (f32[8,128]{1,0:T(8,128)S(1)}, f32[8,128]{1,0:T(8,128)S(1)}, u32[]{:S(2)}, u32[]{:S(2)}) collective-permute-start(f32[8,128]{1,0:T(8,128)S(1)} %get-tuple-element.70), channel_id=1, source_target_pairs={{0,3},{1,2},{2,1},{3,0},{4,7},{5,6},{6,5},{7,4},{8,11},{9,10},{10,... | collective-permute-start | bytes 12296 | tf_op jit(solution)/shard_map/ppermute | solution.py:250
  91.5 6.2 %collective-permute-start.18 = (f32[8,128]{1,0:T(8,128)S(1)}, f32[8,128]{1,0:T(8,128)S(1)}, u32[]{:S(2)}, u32[]{:S(2)}) collective-permute-start(f32[8,128]{1,0:T(8,128)S(1)} %get-tuple-element.71), channel_id=1, source_target_pairs={{0,4},{1,5},{2,6},{3,7},{4,0},{5,1},{6,2},{7,3},{8,12},{9,13},{10,... | collective-permute-start | bytes 12296 | tf_op jit(solution)/shard_map/ppermute | solution.py:250
  93.1 4.8 %collective-permute-start.19 = (f32[8,128]{1,0:T(8,128)S(1)}, f32[8,128]{1,0:T(8,128)S(1)}, u32[]{:S(2)}, u32[]{:S(2)}) collective-permute-start(f32[8,128]{1,0:T(8,128)S(1)} %get-tuple-element.72), channel_id=1, source_target_pairs={{0,5},{1,4},{2,7},{3,6},{4,1},{5,0},{6,3},{7,2},{8,13},{9,12},{10,... | collective-permute-start | bytes 12296 | tf_op jit(solution)/shard_map/ppermute | solution.py:250
  94.4 4.0 %collective-permute-start.20 = (f32[8,128]{1,0:T(8,128)S(1)}, f32[8,128]{1,0:T(8,128)S(1)}, u32[]{:S(2)}, u32[]{:S(2)}) collective-permute-start(f32[8,128]{1,0:T(8,128)S(1)} %get-tuple-element.73), channel_id=1, source_target_pairs={{0,6},{1,7},{2,4},{3,5},{4,2},{5,3},{6,0},{7,1},{8,14},{9,15},{10,... | collective-permute-start | bytes 12296 | tf_op jit(solution)/shard_map/ppermute | solution.py:250
  96.8 4.2 %collective-permute-start.21 = (f32[8,128]{1,0:T(8,128)S(1)}, f32[8,128]{1,0:T(8,128)S(1)}, u32[]{:S(2)}, u32[]{:S(2)}) collective-permute-start(f32[8,128]{1,0:T(8,128)S(1)} %get-tuple-element.74), channel_id=1, source_target_pairs={{0,7},{1,6},{2,5},{3,4},{4,3},{5,2},{6,1},{7,0},{8,15},{9,14},{10,... | collective-permute-start | bytes 12296 | tf_op jit(solution)/shard_map/ppermute | solution.py:250

commit v2 on v1

--- a/solution.py
+++ b/solution.py
@@ -74,17 +74,25 @@
             out_ref[step, zlo] = held[zlo, pl.ds(row, SUB)]
 
 
-def pair_kernel(near_ref, other_ref, *outs):
-    for step in range(YC):
-        outs[step][0] = near_ref[step]
-        outs[step][1] = other_ref[step]
+def pair_kernel(near_ref, other_ref, same_ref, cross_ref):
+    for step in range(Y):
+        for core, out_ref in enumerate((same_ref, cross_ref)):
+            out_ref[step, 0] = near_ref[step * CORE + core]
+            out_ref[step, 1] = other_ref[step * CORE + core]
+
+
+def join_kernel(same_ref, cross_ref, *outs):
+    for step in range(Y):
+        outs[step][0] = same_ref[step]
+        outs[step][1] = cross_ref[step]
 
 
 def route_kernel(x_ref, yc_ref, m0, m1, m2, m3, *refs):
-    pieces, out_ref, held = refs[:YC], refs[YC], refs[YC + 1]
-    for step in range(YC):
-        for zhi in range(ZHI):
-            held[zhi * YC + step] = pieces[step][zhi]
+    pieces, out_ref, held = refs[:Y], refs[Y], refs[Y + 1]
+    for step in range(Y):
+        for core in range(CORE):
+            for zhi in range(ZHI):
+                held[zhi * YC + step * CORE + core] = pieces[step][core, zhi]
     for step, masks in enumerate((m0, m1, m2, m3)):
         base = lax.rem(x_ref[0] + step, X) * YC
         for slot in range(REGIONS - 1):
@@ -283,7 +291,7 @@
         [pltpu.VMEM((ZLO, vecs, LANE), jnp.float32), pltpu.SemaphoreType.DMA((ZLO,))],
         SMALL,
     )(x, yc, own)
-    other = lax.ppermute(near, "zhi", [(0, 1), (1, 0)])
+    other = lax.ppermute(near, ("zlo", "zhi"), [(i, ZLO * ZHI - 1 - i) for i in range(ZLO * ZHI)])
     masks = [matchings] + [
         lax.ppermute(matchings, "x", [(i, (i - step) % X) for i in range(X)])
         for step in range(1, X)
@@ -297,12 +305,15 @@
         half,
     )(*ids, tile_set, own)
     parts = exchange(parts, FAN_AXES)
-    pieces = local(pair_kernel, [(ZHI, *piece)] * YC, [VMEM] * 2, limit=SMALL)(near, other)
-    pieces = swaps(pieces, YC_AXES, YC)
+    side = (Y, ZHI, *piece)
+    same, cross = local(pair_kernel, [side] * CORE, [VMEM] * 2, limit=SMALL)(near, other)
+    cross = lax.ppermute(cross, "core", [(0, 1), (1, 0)])
+    pieces = local(join_kernel, [(CORE, ZHI, *piece)] * Y, [VMEM] * 2, limit=SMALL)(same, cross)
+    pieces = swaps(pieces, "y", Y)
     (wanted,) = local(
         route_kernel,
         [(FAN, REGIONS - 1, *piece)],
-        [SMEM] * 6 + [VMEM] * YC,
+        [SMEM] * 6 + [VMEM] * Y,
         [pltpu.VMEM((OWN, *piece), jnp.float32)],
         SMALL,
     )(x, yc, *masks, *pieces)

time: 105 us -> 99.8 us (0.950)
  starting transfers between devices: 66.9 us -> 55.3 us
  waiting for transfers between devices: 22.2 us -> 28.2 us
    ppermute x17 -> x13, starting transfers between devices: 26.7 us -> 17 us  [swaps(): lax.ppermute(arrays[step], axes, [(i, i ^ step) for i in range(count)])]
    ppermute x1 -> x2, waiting for transfers between devices: 3.64 us -> 7.44 us  [the longest x1 6.45 us: on_device(): lax.ppermute(near, ('zlo', 'zhi'), [(i, ZLO * ZHI - 1 - i) for i in range...]
    ppermute x1, starting transfers between devices: 7 us -> 3.31 us  [on_device(): other = lax.ppermute(other, 'zhi', [(0, 1), (1, 0)])]
    ppermute x17 -> x13, waiting for transfers between devices: 11.2 us -> 7.69 us  [swaps(): lax.ppermute(arrays[step], axes, [(i, i ^ step) for i in range(count)])]
    all_to_all x3, waiting for transfers between devices: 3.45 us -> 6.17 us  [exchange(): return lax.all_to_all(value, axes, 0, 0, tiled=False)]
    ppermute x1, waiting for transfers between devices: 3.72 us -> 5.43 us  [on_device(): other = lax.ppermute(other, 'zhi', [(0, 1), (1, 0)])]
    ppermute x3, waiting for transfers between devices: 0.24 us -> 1.48 us  [on_device(): lax.ppermute(matchings, 'x', [(i, (i - step) % X) for i in range(X)])]
    all_to_all x3, starting transfers between devices: 21.4 us -> 22.6 us  [exchange(): return lax.all_to_all(value, axes, 0, 0, tiled=False)]
  transfers between devices with their start and end apart: 25 -> 22, of which waited for: 13 -> 11; matrix products, arithmetic and copies ran while one was open for 0% -> 0% of each run, Pallas kernels for 3% -> 3%
where the time goes in v2:
time: 99.8 us; the launch traced here: 99.2 us
  starting transfers between devices  55.3 us (55%)
  waiting for transfers between devices  28.2 us (28%)
  Pallas kernels  14.8 us (15%)
    all_to_all x3, starting transfers between devices, exchange(): return lax.all_to_all(value, axes, 0, 0, tiled=False)  22.6 us
    ppermute x13, starting transfers between devices, swaps(): lax.ppermute(arrays[step], axes, [(i, i ^ step) for i in range(count)])  17 us
    ppermute x13, waiting for transfers between devices, swaps(): lax.ppermute(arrays[step], axes, [(i, i ^ step) for i in range(count)])  7.69 us
    ppermute x1, waiting for transfers between devices, on_device(): lax.ppermute(near, ('zlo', 'zhi'), [(i, ZLO * ZHI - 1 - i) for i in range...  6.45 us
    ppermute x1, starting transfers between devices, on_device(): lax.ppermute(near, ('zlo', 'zhi'), [(i, ZLO * ZHI - 1 - i) for i in range...  6.44 us
    all_to_all x3, waiting for transfers between devices, exchange(): return lax.all_to_all(value, axes, 0, 0, tiled=False)  6.17 us
    pallas_call x1, Pallas kernels, on_device(): local(columns_kernel, [(FAN, REGIONS - 1, *piece), (blocks, vecs, LANE)],...  5.76 us
    ppermute x1, waiting for transfers between devices, on_device(): other = lax.ppermute(other, 'zhi', [(0, 1), (1, 0)])  5.43 us
  transfers between devices with their start and end apart: 22, of which 11 were waited for; matrix products, arithmetic and copies ran while one was open for 0% of the time, Pallas kernels for 3%

profile of v2, /device:TPU:1, one launch (start us, length us, event | category | flops | bytes accessed | tf_op | source)
XLA Modules:
  0.0 99.2 jit_solution(15739814744927527761)
XLA Ops:
  0.7 5.8 %shard_map.64 = (f32[32,3,4,8,128]{4,3,2,1,0:T(8,128)}, f32[16,64,128]{2,1,0:T(8,128)}) custom-call(s32[128]{0:T(128)} %bitcast.14, s32[128]{0:T(128)} %bitcast.16, s32[1]{0:T(128)} %bitcast.9.count, f32[128,128,128]{2,1,0:T(8,128)} %bitcast.18, f32[64,2048]{1,0:T(8,128)} %bitcast.11), custom_call_target="tpu_custom_call" | custom-call | flops 805306368 | bytes 8388608 | tf_op jit(solution)/shard_map/pallas_call | solution.py:299
  6.4 8.7 %all-to-all-start = ((f32[32,3,4,8,128]{4,3,2,1,0:T(8,128)}), f32[32,3,4,8,128]{4,3,2,1,0:T(8,128)S(1)}, u32[]{:S(2)}, u32[]{:S(2)}) async-start(f32[32,3,4,8,128]{4,3,2,1,0:T(8,128)} %get-tuple-element.38), calls=%async_computation | async-start | bytes 3145728 | tf_op jit(solution)/shard_map/all_to_all | solution.py:240
  15.3 6.4 %collective-permute-start.3 = (f32[8,4,8,128]{3,2,1,0:T(8,128)S(1)}, f32[8,4,8,128]{3,2,1,0:T(8,128)S(1)}, u32[]{:S(2)}, u32[]{:S(2)}) collective-permute-start(f32[8,4,8,128]{3,2,1,0:T(8,128)S(1)} %shard_map.65.near_ref), channel_id=1, source_target_pairs={{0,200},{8,192},{64,136},{72,128},{128,72},{136,64},{192,8},{200,0... | collective-permute-start | bytes 393224 | tf_op jit(solution)/shard_map/ppermute | solution.py:294
  21.7 6.4 %collective-permute-done.3.other_ref = f32[8,4,8,128]{3,2,1,0:T(8,128)S(1)} collective-permute-done((f32[8,4,8,128]{3,2,1,0:T(8,128)S(1)}, f32[8,4,8,128]{3,2,1,0:T(8,128)S(1)}, u32[]{:S(2)}, u32[]{:S(2)}) %collective-permute-start.3) | collective-permute-done | bytes 131104 | tf_op jit(solution)/shard_map/ppermute | solution.py:294
  28.2 0.9 collective-permute-start.4
  29.1 1.0 collective-permute-done.4.cross_ref
  30.1 1.4 %collective-permute-start.5 = (f32[2,2,4,8,128]{4,3,2,1,0:T(8,128)S(1)}, f32[2,2,4,8,128]{4,3,2,1,0:T(8,128)S(1)}, u32[]{:S(2)}, u32[]{:S(2)}) collective-permute-start(f32[2,2,4,8,128]{4,3,2,1,0:T(8,128)S(1)} %get-tuple-element.42), channel_id=1, source_target_pairs={{0,2},{2,0},{4,6},{6,4},{1,3},{3,1},{5,7},{7,5},{8,10},{10,8},{12,... | collective-permute-start | bytes 196616 | tf_op jit(solution)/shard_map/ppermute | solution.py:258
  31.6 2.4 %collective-permute-start.6 = (f32[2,2,4,8,128]{4,3,2,1,0:T(8,128)S(1)}, f32[2,2,4,8,128]{4,3,2,1,0:T(8,128)S(1)}, u32[]{:S(2)}, u32[]{:S(2)}) collective-permute-start(f32[2,2,4,8,128]{4,3,2,1,0:T(8,128)S(1)} %get-tuple-element.43), channel_id=1, source_target_pairs={{0,4},{2,6},{4,0},{6,2},{1,5},{3,7},{5,1},{7,3},{8,12},{10,14},{12... | collective-permute-start | bytes 196616 | tf_op jit(solution)/shard_map/ppermute | solution.py:258
  34.1 1.4 %collective-permute-start.2 = (s32[1,3]{1,0:T(1,128)S(1)}, s32[1,3]{1,0:T(1,128)S(1)}, u32[]{:S(2)}, u32[]{:S(2)}) collective-permute-start(s32[1,3]{1,0:T(1,128)S(1)} %copy-done.4), channel_id=1, source_target_pairs={{0,16},{16,32},{32,48},{48,0},{1,17},{17,33},{33,49},{49,1},{2,18}... | collective-permute-start | bytes 44 | tf_op jit(solution)/shard_map/ppermute | solution.py:296
  35.4 2.4 %collective-permute-start.1 = (s32[1,3]{1,0:T(1,128)S(1)}, s32[1,3]{1,0:T(1,128)S(1)}, u32[]{:S(2)}, u32[]{:S(2)}) collective-permute-start(s32[1,3]{1,0:T(1,128)S(1)} %copy-done.4), channel_id=1, source_target_pairs={{0,32},{16,48},{32,0},{48,16},{1,33},{17,49},{33,1},{49,17},{2,34}... | collective-permute-start | bytes 44 | tf_op jit(solution)/shard_map/ppermute | solution.py:296
  37.9 1.2 %collective-permute-start = (s32[1,3]{1,0:T(1,128)S(1)}, s32[1,3]{1,0:T(1,128)S(1)}, u32[]{:S(2)}, u32[]{:S(2)}) collective-permute-start(s32[1,3]{1,0:T(1,128)S(1)} %copy-done.4), channel_id=1, source_target_pairs={{0,48},{16,0},{32,16},{48,32},{1,49},{17,1},{33,17},{49,33},{2,50}... | collective-permute-start | bytes 44 | tf_op jit(solution)/shard_map/ppermute | solution.py:296
  39.6 0.9 collective-permute-done.m1
  40.6 1.8 %shard_map.68 = f32[32,3,4,8,128]{4,3,2,1,0:T(8,128)} custom-call(s32[1]{0:T(128)} %bitcast.6.x_ref, s32[1]{0:T(128)} %bitcast.yc_ref, s32[1,3]{1,0:T(1,128)S(1)} %copy-done.4, s32[1,3]{1,0:T(1,128)S(1)} %collective-permute-done.m1, s32[1,3]{1,0:T(1,128)S(1)} %collective-permute-done.1.m2, s32[1,3]{1,0:T(1,128)S(1)} %collective-permute-done.2.m3, ...), custom_call_target="tpu_custom_call" | custom-call | tf_op jit(solution)/shard_map/pallas_call | solution.py:313
  42.4 9.6 %all-to-all-start.1 = ((f32[32,3,4,8,128]{4,3,2,1,0:T(8,128)}), f32[32,3,4,8,128]{4,3,2,1,0:T(8,128)}, u32[]{:S(2)}, u32[]{:S(2)}) async-start(f32[32,3,4,8,128]{4,3,2,1,0:T(8,128)} %shard_map.68), calls=%async_computation.1 | async-start | bytes 3145728 | tf_op jit(solution)/shard_map/all_to_all | solution.py:240
  52.0 1.0 %shard_map.70 = (f32[4,8,8,128]{3,2,1,0:T(8,128)S(1)}, f32[4,8,8,128]{3,2,1,0:T(8,128)S(1)}) custom-call(s32[1]{0:T(128)} %bitcast.6.x_ref, s32[1]{0:T(128)} %bitcast.yc_ref, s32[1]{0:T(128)} %bitcast.7.zlo_ref, s32[1,3]{1,0:T(1,128)S(1)} %copy-done.4, s32[1,3]{1,0:T(1,128)S(1)} %collective-permute-done.m1, s32[1,3]{1,0:T(1,128)S(1)} %collective-permute-done.1.m2, ...), custom_call_target="tpu_custom_call" | custom-call | tf_op jit(solution)/shard_map/pallas_call | solution.py:323
  53.1 3.3 %collective-permute-start.8 = (f32[4,8,8,128]{3,2,1,0:T(8,128)S(1)}, f32[4,8,8,128]{3,2,1,0:T(8,128)S(1)}, u32[]{:S(2)}, u32[]{:S(2)}) collective-permute-start(f32[4,8,8,128]{3,2,1,0:T(8,128)S(1)} %get-tuple-element.49), channel_id=1, source_target_pairs={{0,8},{8,0},{1,9},{9,1},{2,10},{10,2},{3,11},{11,3},{4,12},{12,4},... | collective-permute-start | bytes 393224 | tf_op jit(solution)/shard_map/ppermute | solution.py:330
  56.4 5.4 %collective-permute-done.8.b_ref = f32[4,8,8,128]{3,2,1,0:T(8,128)S(1)} collective-permute-done((f32[4,8,8,128]{3,2,1,0:T(8,128)S(1)}, f32[4,8,8,128]{3,2,1,0:T(8,128)S(1)}, u32[]{:S(2)}, u32[]{:S(2)}) %collective-permute-start.8) | collective-permute-done | bytes 131104 | tf_op jit(solution)/shard_map/ppermute | solution.py:330
  61.9 1.8 %collective-permute-start.10 = (f32[8,8,128]{2,1,0:T(8,128)S(1)}, f32[8,8,128]{2,1,0:T(8,128)S(1)}, u32[]{:S(2)}, u32[]{:S(2)}) collective-permute-start(f32[8,8,128]{2,1,0:T(8,128)S(1)} %get-tuple-element.52), channel_id=1, source_target_pairs={{0,128},{64,192},{128,0},{192,64},{1,129},{65,193},{129,1},{193,65... | collective-permute-start | bytes 98312 | tf_op jit(solution)/shard_map/ppermute | solution.py:258
  63.7 1.7 %collective-permute-start.11 = (f32[8,8,128]{2,1,0:T(8,128)S(1)}, f32[8,8,128]{2,1,0:T(8,128)S(1)}, u32[]{:S(2)}, u32[]{:S(2)}) collective-permute-start(f32[8,8,128]{2,1,0:T(8,128)S(1)} %get-tuple-element.53), channel_id=1, source_target_pairs={{0,192},{64,128},{128,64},{192,0},{1,193},{65,129},{129,65},{193,1... | collective-permute-start | bytes 98312 | tf_op jit(solution)/shard_map/ppermute | solution.py:258
  65.5 0.8 collective-permute-done.10.c_ref
  66.3 2.4 %collective-permute-done.11.d_ref = f32[8,8,128]{2,1,0:T(8,128)S(1)} collective-permute-done((f32[8,8,128]{2,1,0:T(8,128)S(1)}, f32[8,8,128]{2,1,0:T(8,128)S(1)}, u32[]{:S(2)}, u32[]{:S(2)}) %collective-permute-start.11) | collective-permute-done | bytes 32800 | tf_op jit(solution)/shard_map/ppermute | solution.py:258
  68.7 6.0 %all-to-all-done.1.far = f32[32,3,4,8,128]{4,3,2,1,0:T(8,128)} async-done(((f32[32,3,4,8,128]{4,3,2,1,0:T(8,128)}), f32[32,3,4,8,128]{4,3,2,1,0:T(8,128)}, u32[]{:S(2)}, u32[]{:S(2)}) %all-to-all-start.1) | async-done | bytes 1572896 | tf_op jit(solution)/shard_map/all_to_all | solution.py:240
  74.7 5.4 %shard_map.69 = f32[16,64,128]{2,1,0:T(8,128)} custom-call(s32[128]{0:T(128)S(1)} %bitcast.15, s32[128]{0:T(128)S(1)} %bitcast.17, s32[1]{0:T(128)} %bitcast.10.count, f32[128,128,128]{2,1,0:T(8,128)} %bitcast.19, f32[64,2048]{1,0:T(8,128)S(1)} %bitcast.13, f32[32,3,4,8,128]{4,3,2,1,0:T(8,128)} %all-to-all-done.1.far, f32[16,64,128]{2,1,0:T(8,128)S(1)} %copy-done.1), custom_call_target="tpu_custom_call" | custom-call | flops 805306368 | bytes 8388608 | tf_op jit(solution)/shard_map/pallas_call | solution.py:334
  80.1 4.3 %all-to-all-start.2 = ((f32[16,64,128]{2,1,0:T(8,128)}), f32[16,64,128]{2,1,0:T(8,128)S(1)}, u32[]{:S(2)}, u32[]{:S(2)}) async-start(f32[16,64,128]{2,1,0:T(8,128)} %shard_map.69), calls=%async_computation.2 | async-start | bytes 1048576 | tf_op jit(solution)/shard_map/all_to_all | solution.py:240
  84.4 0.8 collective-permute-start.12
  85.2 1.2 %collective-permute-start.13 = (f32[8,128]{1,0:T(8,128)S(1)}, f32[8,128]{1,0:T(8,128)S(1)}, u32[]{:S(2)}, u32[]{:S(2)}) collective-permute-start(f32[8,128]{1,0:T(8,128)S(1)} %get-tuple-element.65), channel_id=1, source_target_pairs={{0,2},{1,3},{2,0},{3,1},{4,6},{5,7},{6,4},{7,5},{8,10},{9,11},{10,... | collective-permute-start | bytes 12296 | tf_op jit(solution)/shard_map/ppermute | solution.py:258
  86.4 0.5 collective-permute-start.14
  87.0 3.1 %collective-permute-start.15 = (f32[8,128]{1,0:T(8,128)S(1)}, f32[8,128]{1,0:T(8,128)S(1)}, u32[]{:S(2)}, u32[]{:S(2)}) collective-permute-start(f32[8,128]{1,0:T(8,128)S(1)} %get-tuple-element.67), channel_id=1, source_target_pairs={{0,4},{1,5},{2,6},{3,7},{4,0},{5,1},{6,2},{7,3},{8,12},{9,13},{10,... | collective-permute-start | bytes 12296 | tf_op jit(solution)/shard_map/ppermute | solution.py:258
  90.3 3.5 %collective-permute-start.17 = (f32[8,128]{1,0:T(8,128)S(1)}, f32[8,128]{1,0:T(8,128)S(1)}, u32[]{:S(2)}, u32[]{:S(2)}) collective-permute-start(f32[8,128]{1,0:T(8,128)S(1)} %get-tuple-element.69), channel_id=1, source_target_pairs={{0,6},{1,7},{2,4},{3,5},{4,2},{5,3},{6,0},{7,1},{8,14},{9,15},{10,... | collective-permute-start | bytes 12296 | tf_op jit(solution)/shard_map/ppermute | solution.py:258
  93.9 0.9 collective-permute-done.16.refs_5_
  94.8 3.5 %collective-permute-done.18.refs_7_ = f32[8,128]{1,0:T(8,128)S(1)} collective-permute-done((f32[8,128]{1,0:T(8,128)S(1)}, f32[8,128]{1,0:T(8,128)S(1)}, u32[]{:S(2)}, u32[]{:S(2)}) %collective-permute-start.18) | collective-permute-done | bytes 4128 | tf_op jit(solution)/shard_map/ppermute | solution.py:258
  98.5 0.7 shard_map.73
  (32 shorter events, 1.4 us)
Async XLA Ops:
  6.4 8.8 %copy-start = (f32[1,64,2048]{2,1,0:T(8,128)S(1)}, f32[1,64,2048]{2,1,0:T(8,128)}, u32[]{:S(2)}) copy-start(f32[1,64,2048]{2,1,0:T(8,128)} %param.6) | copy-start | bytes 1572868
  6.4 27.6 %copy-start.4 = (s32[1,3]{1,0:T(1,128)S(1)}, s32[1,3]{1,0:T(1,128)}, u32[]{:S(2)}) copy-start(s32[1,3]{1,0:T(1,128)} %m0.3) | copy-start | bytes 40
  6.4 36.0 %all-to-all-start = ((f32[32,3,4,8,128]{4,3,2,1,0:T(8,128)}), f32[32,3,4,8,128]{4,3,2,1,0:T(8,128)S(1)}, u32[]{:S(2)}, u32[]{:S(2)}) async-start(f32[32,3,4,8,128]{4,3,2,1,0:T(8,128)} %get-tuple-element.38), calls=%async_computation | async-start | bytes 3145728 | tf_op jit(solution)/shard_map/all_to_all | solution.py:240
  15.3 12.9 %collective-permute-start.3 = (f32[8,4,8,128]{3,2,1,0:T(8,128)S(1)}, f32[8,4,8,128]{3,2,1,0:T(8,128)S(1)}, u32[]{:S(2)}, u32[]{:S(2)}) collective-permute-start(f32[8,4,8,128]{3,2,1,0:T(8,128)S(1)} %shard_map.65.near_ref), channel_id=1, source_target_pairs={{0,200},{8,192},{64,136},{72,128},{128,72},{136,64},{192,8},{200,0... | collective-permute-start | bytes 393224 | tf_op jit(solution)/shard_map/ppermute | solution.py:294
  28.2 1.9 %collective-permute-start.4 = (f32[4,2,4,8,128]{4,3,2,1,0:T(8,128)S(1)}, f32[4,2,4,8,128]{4,3,2,1,0:T(8,128)S(1)}, u32[]{:S(2)}, u32[]{:S(2)}) collective-permute-start(f32[4,2,4,8,128]{4,3,2,1,0:T(8,128)S(1)} %get-tuple-element.40), channel_id=1, source_target_pairs={{0,1},{1,0},{2,3},{3,2},{4,5},{5,4},{6,7},{7,6},{8,9},{9,8},{10,11... | collective-permute-start | bytes 393224 | tf_op jit(solution)/shard_map/ppermute | solution.py:310
  30.1 10.5 %collective-permute-start.5 = (f32[2,2,4,8,128]{4,3,2,1,0:T(8,128)S(1)}, f32[2,2,4,8,128]{4,3,2,1,0:T(8,128)S(1)}, u32[]{:S(2)}, u32[]{:S(2)}) collective-permute-start(f32[2,2,4,8,128]{4,3,2,1,0:T(8,128)S(1)} %get-tuple-element.42), channel_id=1, source_target_pairs={{0,2},{2,0},{4,6},{6,4},{1,3},{3,1},{5,7},{7,5},{8,10},{10,8},{12,... | collective-permute-start | bytes 196616 | tf_op jit(solution)/shard_map/ppermute | solution.py:258
  31.6 9.0 %collective-permute-start.6 = (f32[2,2,4,8,128]{4,3,2,1,0:T(8,128)S(1)}, f32[2,2,4,8,128]{4,3,2,1,0:T(8,128)S(1)}, u32[]{:S(2)}, u32[]{:S(2)}) collective-permute-start(f32[2,2,4,8,128]{4,3,2,1,0:T(8,128)S(1)} %get-tuple-element.43), channel_id=1, source_target_pairs={{0,4},{2,6},{4,0},{6,2},{1,5},{3,7},{5,1},{7,3},{8,12},{10,14},{12... | collective-permute-start | bytes 196616 | tf_op jit(solution)/shard_map/ppermute | solution.py:258
  34.0 6.6 %collective-permute-start.7 = (f32[2,2,4,8,128]{4,3,2,1,0:T(8,128)S(1)}, f32[2,2,4,8,128]{4,3,2,1,0:T(8,128)S(1)}, u32[]{:S(2)}, u32[]{:S(2)}) collective-permute-start(f32[2,2,4,8,128]{4,3,2,1,0:T(8,128)S(1)} %get-tuple-element.44), channel_id=1, source_target_pairs={{0,6},{2,4},{4,2},{6,0},{1,7},{3,5},{5,3},{7,1},{8,14},{10,12},{12... | collective-permute-start | bytes 196616 | tf_op jit(solution)/shard_map/ppermute | solution.py:258
  34.1 3.8 %collective-permute-start.2 = (s32[1,3]{1,0:T(1,128)S(1)}, s32[1,3]{1,0:T(1,128)S(1)}, u32[]{:S(2)}, u32[]{:S(2)}) collective-permute-start(s32[1,3]{1,0:T(1,128)S(1)} %copy-done.4), channel_id=1, source_target_pairs={{0,16},{16,32},{32,48},{48,0},{1,17},{17,33},{33,49},{49,1},{2,18}... | collective-permute-start | bytes 44 | tf_op jit(solution)/shard_map/ppermute | solution.py:296
  35.4 4.2 %collective-permute-start.1 = (s32[1,3]{1,0:T(1,128)S(1)}, s32[1,3]{1,0:T(1,128)S(1)}, u32[]{:S(2)}, u32[]{:S(2)}) collective-permute-start(s32[1,3]{1,0:T(1,128)S(1)} %copy-done.4), channel_id=1, source_target_pairs={{0,32},{16,48},{32,0},{48,16},{1,33},{17,49},{33,1},{49,17},{2,34}... | collective-permute-start | bytes 44 | tf_op jit(solution)/shard_map/ppermute | solution.py:296
  37.9 2.7 %collective-permute-start = (s32[1,3]{1,0:T(1,128)S(1)}, s32[1,3]{1,0:T(1,128)S(1)}, u32[]{:S(2)}, u32[]{:S(2)}) collective-permute-start(s32[1,3]{1,0:T(1,128)S(1)} %copy-done.4), channel_id=1, source_target_pairs={{0,48},{16,0},{32,16},{48,32},{1,49},{17,1},{33,17},{49,33},{2,50}... | collective-permute-start | bytes 44 | tf_op jit(solution)/shard_map/ppermute | solution.py:296
  42.4 32.3 %all-to-all-start.1 = ((f32[32,3,4,8,128]{4,3,2,1,0:T(8,128)}), f32[32,3,4,8,128]{4,3,2,1,0:T(8,128)}, u32[]{:S(2)}, u32[]{:S(2)}) async-start(f32[32,3,4,8,128]{4,3,2,1,0:T(8,128)} %shard_map.68), calls=%async_computation.1 | async-start | bytes 3145728 | tf_op jit(solution)/shard_map/all_to_all | solution.py:240
  52.0 22.7 %copy-start.1 = (f32[16,64,128]{2,1,0:T(8,128)S(1)}, f32[16,64,128]{2,1,0:T(8,128)}, u32[]{:S(2)}) copy-start(f32[16,64,128]{2,1,0:T(8,128)} %get-tuple-element.46.mine) | copy-start | bytes 1572868
  52.0 22.7 %copy-start.2 = (s32[1,1,128]{2,1,0:T(1,128)S(1)}, s32[1,1,128]{2,1,0:T(1,128)}, u32[]{:S(2)}) copy-start(s32[1,1,128]{2,1,0:T(1,128)} %param.8) | copy-start | bytes 1540
  52.0 22.7 %copy-start.3 = (s32[1,1,128]{2,1,0:T(1,128)S(1)}, s32[1,1,128]{2,1,0:T(1,128)}, u32[]{:S(2)}) copy-start(s32[1,1,128]{2,1,0:T(1,128)} %param.9) | copy-start | bytes 1540
  53.1 8.7 %collective-permute-start.8 = (f32[4,8,8,128]{3,2,1,0:T(8,128)S(1)}, f32[4,8,8,128]{3,2,1,0:T(8,128)S(1)}, u32[]{:S(2)}, u32[]{:S(2)}) collective-permute-start(f32[4,8,8,128]{3,2,1,0:T(8,128)S(1)} %get-tuple-element.49), channel_id=1, source_target_pairs={{0,8},{8,0},{1,9},{9,1},{2,10},{10,2},{3,11},{11,3},{4,12},{12,4},... | collective-permute-start | bytes 393224 | tf_op jit(solution)/shard_map/ppermute | solution.py:330
  61.8 3.6 %collective-permute-start.9 = (f32[8,8,128]{2,1,0:T(8,128)S(1)}, f32[8,8,128]{2,1,0:T(8,128)S(1)}, u32[]{:S(2)}, u32[]{:S(2)}) collective-permute-start(f32[8,8,128]{2,1,0:T(8,128)S(1)} %get-tuple-element.51), channel_id=1, source_target_pairs={{0,64},{64,0},{128,192},{192,128},{1,65},{65,1},{129,193},{193,129... | collective-permute-start | bytes 98312 | tf_op jit(solution)/shard_map/ppermute | solution.py:258
  61.9 4.3 %collective-permute-start.10 = (f32[8,8,128]{2,1,0:T(8,128)S(1)}, f32[8,8,128]{2,1,0:T(8,128)S(1)}, u32[]{:S(2)}, u32[]{:S(2)}) collective-permute-start(f32[8,8,128]{2,1,0:T(8,128)S(1)} %get-tuple-element.52), channel_id=1, source_target_pairs={{0,128},{64,192},{128,0},{192,64},{1,129},{65,193},{129,1},{193,65... | collective-permute-start | bytes 98312 | tf_op jit(solution)/shard_map/ppermute | solution.py:258
  63.7 5.0 %collective-permute-start.11 = (f32[8,8,128]{2,1,0:T(8,128)S(1)}, f32[8,8,128]{2,1,0:T(8,128)S(1)}, u32[]{:S(2)}, u32[]{:S(2)}) collective-permute-start(f32[8,8,128]{2,1,0:T(8,128)S(1)} %get-tuple-element.53), channel_id=1, source_target_pairs={{0,192},{64,128},{128,64},{192,0},{1,193},{65,129},{129,65},{193,1... | collective-permute-start | bytes 98312 | tf_op jit(solution)/shard_map/ppermute | solution.py:258
  80.1 18.4 %all-to-all-start.2 = ((f32[16,64,128]{2,1,0:T(8,128)}), f32[16,64,128]{2,1,0:T(8,128)S(1)}, u32[]{:S(2)}, u32[]{:S(2)}) async-start(f32[16,64,128]{2,1,0:T(8,128)} %shard_map.69), calls=%async_computation.2 | async-start | bytes 1048576 | tf_op jit(solution)/shard_map/all_to_all | solution.py:240
  84.4 5.8 %collective-permute-start.12 = (f32[8,128]{1,0:T(8,128)S(1)}, f32[8,128]{1,0:T(8,128)S(1)}, u32[]{:S(2)}, u32[]{:S(2)}) collective-permute-start(f32[8,128]{1,0:T(8,128)S(1)} %get-tuple-element.64), channel_id=1, source_target_pairs={{0,1},{1,0},{2,3},{3,2},{4,5},{5,4},{6,7},{7,6},{8,9},{9,8},{10,11... | collective-permute-start | bytes 12296 | tf_op jit(solution)/shard_map/ppermute | solution.py:258
  85.2 8.6 %collective-permute-start.13 = (f32[8,128]{1,0:T(8,128)S(1)}, f32[8,128]{1,0:T(8,128)S(1)}, u32[]{:S(2)}, u32[]{:S(2)}) collective-permute-start(f32[8,128]{1,0:T(8,128)S(1)} %get-tuple-element.65), channel_id=1, source_target_pairs={{0,2},{1,3},{2,0},{3,1},{4,6},{5,7},{6,4},{7,5},{8,10},{9,11},{10,... | collective-permute-start | bytes 12296 | tf_op jit(solution)/shard_map/ppermute | solution.py:258
  86.4 7.5 %collective-permute-start.14 = (f32[8,128]{1,0:T(8,128)S(1)}, f32[8,128]{1,0:T(8,128)S(1)}, u32[]{:S(2)}, u32[]{:S(2)}) collective-permute-start(f32[8,128]{1,0:T(8,128)S(1)} %get-tuple-element.66), channel_id=1, source_target_pairs={{0,3},{1,2},{2,1},{3,0},{4,7},{5,6},{6,5},{7,4},{8,11},{9,10},{10,... | collective-permute-start | bytes 12296 | tf_op jit(solution)/shard_map/ppermute | solution.py:258
  87.0 6.9 %collective-permute-start.15 = (f32[8,128]{1,0:T(8,128)S(1)}, f32[8,128]{1,0:T(8,128)S(1)}, u32[]{:S(2)}, u32[]{:S(2)}) collective-permute-start(f32[8,128]{1,0:T(8,128)S(1)} %get-tuple-element.67), channel_id=1, source_target_pairs={{0,4},{1,5},{2,6},{3,7},{4,0},{5,1},{6,2},{7,3},{8,12},{9,13},{10,... | collective-permute-start | bytes 12296 | tf_op jit(solution)/shard_map/ppermute | solution.py:258
  90.1 4.8 %collective-permute-start.16 = (f32[8,128]{1,0:T(8,128)S(1)}, f32[8,128]{1,0:T(8,128)S(1)}, u32[]{:S(2)}, u32[]{:S(2)}) collective-permute-start(f32[8,128]{1,0:T(8,128)S(1)} %get-tuple-element.68), channel_id=1, source_target_pairs={{0,5},{1,4},{2,7},{3,6},{4,1},{5,0},{6,3},{7,2},{8,13},{9,12},{10,... | collective-permute-start | bytes 12296 | tf_op jit(solution)/shard_map/ppermute | solution.py:258
  90.3 4.6 %collective-permute-start.17 = (f32[8,128]{1,0:T(8,128)S(1)}, f32[8,128]{1,0:T(8,128)S(1)}, u32[]{:S(2)}, u32[]{:S(2)}) collective-permute-start(f32[8,128]{1,0:T(8,128)S(1)} %get-tuple-element.69), channel_id=1, source_target_pairs={{0,6},{1,7},{2,4},{3,5},{4,2},{5,3},{6,0},{7,1},{8,14},{9,15},{10,... | collective-permute-start | bytes 12296 | tf_op jit(solution)/shard_map/ppermute | solution.py:258
  93.8 4.5 %collective-permute-start.18 = (f32[8,128]{1,0:T(8,128)S(1)}, f32[8,128]{1,0:T(8,128)S(1)}, u32[]{:S(2)}, u32[]{:S(2)}) collective-permute-start(f32[8,128]{1,0:T(8,128)S(1)} %get-tuple-element.70), channel_id=1, source_target_pairs={{0,7},{1,6},{2,5},{3,4},{4,3},{5,2},{6,1},{7,0},{8,15},{9,14},{10,... | collective-permute-start | bytes 12296 | tf_op jit(solution)/shard_map/ppermute | solution.py:258

commit v3 on v2

--- a/solution.py
+++ b/solution.py
@@ -88,17 +88,23 @@
 
 
 def route_kernel(x_ref, yc_ref, m0, m1, m2, m3, *refs):
-    pieces, out_ref, held = refs[:Y], refs[Y], refs[Y + 1]
+    pieces, (out, held, out_ref, sems) = refs[:Y], refs[Y:]
     for step in range(Y):
         for core in range(CORE):
             for zhi in range(ZHI):
                 held[zhi * YC + step * CORE + core] = pieces[step][core, zhi]
+    results = []
     for step, masks in enumerate((m0, m1, m2, m3)):
         base = lax.rem(x_ref[0] + step, X) * YC
         for slot in range(REGIONS - 1):
             mask = masks[0, slot]
             for part in range(YC):
                 out_ref[base + part, slot] = held[(part ^ yc_ref[0]) ^ mask]
+        here = pl.ds(base, YC)
+        results.append(pltpu.make_async_copy(out_ref.at[here], out.at[here], sems.at[step]))
+        results[-1].start()
+    for copy in results:
+        copy.wait()
 
 
 def collect_kernel(x_ref, yc_ref, zlo_ref, m0, m1, m2, m3, parts_ref, near_ref, other_ref, sums):
@@ -171,7 +177,9 @@
             done = here // size * size
 
 
-def columns_kernel(rows, cols, count, tiles, own, out_ref, self_ref, held, table, sums, near, sems):
+def columns_kernel(
+    rows, cols, count, tiles, own, out, self_out, held, table, sums, near, out_ref, sems, out_sems
+):
     first = pltpu.make_async_copy(own, near, sems.at[sems.shape[0] - 1])
     first.start()
     copies = fetch(tiles, held, sems)
@@ -190,13 +198,20 @@
             sums[col] += done[k]
 
     each_group(copies, count[0], group)
-    self_ref[...] = sums[:blocks]
-    for slot in range(REGIONS - 1):
-        for block in range(blocks):
-            zlo, x = divmod(block, X)
-            value = sums[(slot + 1) * blocks + block]
-            for part in range(YC):
-                out_ref[x * YC + part, slot, zlo] = value[part * SUB : (part + 1) * SUB]
+    mine = pltpu.make_async_copy(sums.at[pl.ds(0, blocks)], self_out, out_sems.at[X])
+    mine.start()
+    results = []
+    for x in range(X):
+        here = pl.ds(x * YC, YC)
+        for slot in range(REGIONS - 1):
+            for zlo in range(blocks // X):
+                value = sums[(slot + 1) * blocks + zlo * X + x]
+                for part in range(YC):
+                    out_ref[x * YC + part, slot, zlo] = value[part * SUB : (part + 1) * SUB]
+        results.append(pltpu.make_async_copy(out_ref.at[here], out.at[here], out_sems.at[x]))
+        results[-1].start()
+    for copy in (mine, *results):
+        copy.wait()
 
 
 def rows_kernel(
@@ -240,13 +255,13 @@
     return lax.all_to_all(value, axes, 0, 0, tiled=False)
 
 
-def local(kernel, outs, specs, scratch=(), limit=None, cost=None):
+def local(kernel, outs, specs, scratch=(), limit=None, cost=None, place=VMEM):
     outs = [jax.ShapeDtypeStruct(shape, jnp.float32) for shape in outs]
     return pl.pallas_call(
         kernel,
         out_shape=outs,
         in_specs=specs,
-        out_specs=[VMEM] * len(outs),
+        out_specs=[place] * len(outs),
         scratch_shapes=scratch,
         compiler_params=pltpu.CompilerParams(vmem_limit_bytes=limit),
         cost_estimate=cost,
@@ -300,9 +315,15 @@
         columns_kernel,
         [(FAN, REGIONS - 1, *piece), (blocks, vecs, LANE)],
         [SMEM] * 3 + [HBM] * 2,
-        tile_scratch(blocks, [(REGIONS * blocks, vecs, LANE), own.shape], 1),
+        [
+            *tile_scratch(
+                blocks, [(REGIONS * blocks, vecs, LANE), own.shape, (FAN, REGIONS - 1, *piece)], 1
+            ),
+            pltpu.SemaphoreType.DMA((X + 1,)),
+        ],
         LARGE,
         half,
+        HBM,
     )(*ids, tile_set, own)
     parts = exchange(parts, FAN_AXES)
     side = (Y, ZHI, *piece)
@@ -314,8 +335,13 @@
         route_kernel,
         [(FAN, REGIONS - 1, *piece)],
         [SMEM] * 6 + [VMEM] * Y,
-        [pltpu.VMEM((OWN, *piece), jnp.float32)],
+        [
+            pltpu.VMEM((OWN, *piece), jnp.float32),
+            pltpu.VMEM((FAN, REGIONS - 1, *piece), jnp.float32),
+            pltpu.SemaphoreType.DMA((X,)),
+        ],
         SMALL,
+        place=HBM,
     )(x, yc, *masks, *pieces)
     parts, wanted = lax.optimization_barrier((parts, wanted))
     far = exchange(wanted, FAN_AXES)

time: 99.8 us -> 99.7 us (level)
  no operation moved by 1% of the time
where the time goes in v3:
time: 99.7 us; the launch traced here: 99.1 us
  starting transfers between devices  55.3 us (55%)
  waiting for transfers between devices  28.2 us (28%)
  Pallas kernels  14.8 us (15%)
    all_to_all x3, starting transfers between devices, exchange(): return lax.all_to_all(value, axes, 0, 0, tiled=False)  22.6 us
    ppermute x13, starting transfers between devices, swaps(): lax.ppermute(arrays[step], axes, [(i, i ^ step) for i in range(count)])  17 us
    ppermute x13, waiting for transfers between devices, swaps(): lax.ppermute(arrays[step], axes, [(i, i ^ step) for i in range(count)])  7.69 us
    ppermute x1, waiting for transfers between devices, on_device(): lax.ppermute(near, ('zlo', 'zhi'), [(i, ZLO * ZHI - 1 - i) for i in range...  6.45 us
    ppermute x1, starting transfers between devices, on_device(): lax.ppermute(near, ('zlo', 'zhi'), [(i, ZLO * ZHI - 1 - i) for i in range...  6.44 us
    all_to_all x3, waiting for transfers between devices, exchange(): return lax.all_to_all(value, axes, 0, 0, tiled=False)  6.17 us
    pallas_call x1, Pallas kernels, on_device(): local(columns_kernel, [(FAN, REGIONS - 1, *piece), (blocks, vecs, LANE)],...  5.73 us
    ppermute x1, waiting for transfers between devices, on_device(): other = lax.ppermute(other, 'zhi', [(0, 1), (1, 0)])  5.43 us
  transfers between devices with their start and end apart: 22, of which 11 were waited for; matrix products, arithmetic and copies ran while one was open for 0% of the time, Pallas kernels for 3%

profile of v3, /device:TPU:1, one launch (start us, length us, event | category | flops | bytes accessed | tf_op | source)
XLA Modules:
  0.0 99.1 jit_solution(2415997501529579793)
XLA Ops:
  0.7 5.7 %shard_map.64 = (f32[32,3,4,8,128]{4,3,2,1,0:T(8,128)}, f32[16,64,128]{2,1,0:T(8,128)}) custom-call(s32[128]{0:T(128)} %bitcast.14, s32[128]{0:T(128)} %bitcast.16, s32[1]{0:T(128)} %bitcast.9.count, f32[128,128,128]{2,1,0:T(8,128)} %bitcast.18, f32[64,2048]{1,0:T(8,128)} %bitcast.11), custom_call_target="tpu_custom_call" | custom-call | flops 805306368 | bytes 8388608 | tf_op jit(solution)/shard_map/pallas_call | solution.py:314
  6.4 8.7 %all-to-all-start = ((f32[32,3,4,8,128]{4,3,2,1,0:T(8,128)}), f32[32,3,4,8,128]{4,3,2,1,0:T(8,128)S(1)}, u32[]{:S(2)}, u32[]{:S(2)}) async-start(f32[32,3,4,8,128]{4,3,2,1,0:T(8,128)} %get-tuple-element.38), calls=%async_computation | async-start | bytes 3145728 | tf_op jit(solution)/shard_map/all_to_all | solution.py:255
  15.3 6.4 %collective-permute-start.3 = (f32[8,4,8,128]{3,2,1,0:T(8,128)S(1)}, f32[8,4,8,128]{3,2,1,0:T(8,128)S(1)}, u32[]{:S(2)}, u32[]{:S(2)}) collective-permute-start(f32[8,4,8,128]{3,2,1,0:T(8,128)S(1)} %shard_map.65.near_ref), channel_id=1, source_target_pairs={{0,200},{8,192},{64,136},{72,128},{128,72},{136,64},{192,8},{200,0... | collective-permute-start | bytes 393224 | tf_op jit(solution)/shard_map/ppermute | solution.py:309
  21.7 6.4 %collective-permute-done.3.other_ref = f32[8,4,8,128]{3,2,1,0:T(8,128)S(1)} collective-permute-done((f32[8,4,8,128]{3,2,1,0:T(8,128)S(1)}, f32[8,4,8,128]{3,2,1,0:T(8,128)S(1)}, u32[]{:S(2)}, u32[]{:S(2)}) %collective-permute-start.3) | collective-permute-done | bytes 131104 | tf_op jit(solution)/shard_map/ppermute | solution.py:309
  28.2 0.9 collective-permute-start.4
  29.1 1.0 collective-permute-done.4.cross_ref
  30.1 1.4 %collective-permute-start.5 = (f32[2,2,4,8,128]{4,3,2,1,0:T(8,128)S(1)}, f32[2,2,4,8,128]{4,3,2,1,0:T(8,128)S(1)}, u32[]{:S(2)}, u32[]{:S(2)}) collective-permute-start(f32[2,2,4,8,128]{4,3,2,1,0:T(8,128)S(1)} %get-tuple-element.42), channel_id=1, source_target_pairs={{0,2},{2,0},{4,6},{6,4},{1,3},{3,1},{5,7},{7,5},{8,10},{10,8},{12,... | collective-permute-start | bytes 196616 | tf_op jit(solution)/shard_map/ppermute | solution.py:273
  31.5 2.4 %collective-permute-start.6 = (f32[2,2,4,8,128]{4,3,2,1,0:T(8,128)S(1)}, f32[2,2,4,8,128]{4,3,2,1,0:T(8,128)S(1)}, u32[]{:S(2)}, u32[]{:S(2)}) collective-permute-start(f32[2,2,4,8,128]{4,3,2,1,0:T(8,128)S(1)} %get-tuple-element.43), channel_id=1, source_target_pairs={{0,4},{2,6},{4,0},{6,2},{1,5},{3,7},{5,1},{7,3},{8,12},{10,14},{12... | collective-permute-start | bytes 196616 | tf_op jit(solution)/shard_map/ppermute | solution.py:273
  34.0 1.4 %collective-permute-start.2 = (s32[1,3]{1,0:T(1,128)S(1)}, s32[1,3]{1,0:T(1,128)S(1)}, u32[]{:S(2)}, u32[]{:S(2)}) collective-permute-start(s32[1,3]{1,0:T(1,128)S(1)} %copy-done.4), channel_id=1, source_target_pairs={{0,16},{16,32},{32,48},{48,0},{1,17},{17,33},{33,49},{49,1},{2,18}... | collective-permute-start | bytes 44 | tf_op jit(solution)/shard_map/ppermute | solution.py:311
  35.4 2.4 %collective-permute-start.1 = (s32[1,3]{1,0:T(1,128)S(1)}, s32[1,3]{1,0:T(1,128)S(1)}, u32[]{:S(2)}, u32[]{:S(2)}) collective-permute-start(s32[1,3]{1,0:T(1,128)S(1)} %copy-done.4), channel_id=1, source_target_pairs={{0,32},{16,48},{32,0},{48,16},{1,33},{17,49},{33,1},{49,17},{2,34}... | collective-permute-start | bytes 44 | tf_op jit(solution)/shard_map/ppermute | solution.py:311
  37.8 1.2 %collective-permute-start = (s32[1,3]{1,0:T(1,128)S(1)}, s32[1,3]{1,0:T(1,128)S(1)}, u32[]{:S(2)}, u32[]{:S(2)}) collective-permute-start(s32[1,3]{1,0:T(1,128)S(1)} %copy-done.4), channel_id=1, source_target_pairs={{0,48},{16,0},{32,16},{48,32},{1,49},{17,1},{33,17},{49,33},{2,50}... | collective-permute-start | bytes 44 | tf_op jit(solution)/shard_map/ppermute | solution.py:311
  39.6 0.9 collective-permute-done.m1
  40.6 1.8 %shard_map.68 = f32[32,3,4,8,128]{4,3,2,1,0:T(8,128)} custom-call(s32[1]{0:T(128)} %bitcast.6.x_ref, s32[1]{0:T(128)} %bitcast.yc_ref, s32[1,3]{1,0:T(1,128)S(1)} %copy-done.4, s32[1,3]{1,0:T(1,128)S(1)} %collective-permute-done.m1, s32[1,3]{1,0:T(1,128)S(1)} %collective-permute-done.1.m2, s32[1,3]{1,0:T(1,128)S(1)} %collective-permute-done.2.m3, ...), custom_call_target="tpu_custom_call" | custom-call | tf_op jit(solution)/shard_map/pallas_call | solution.py:334
  42.4 9.6 %all-to-all-start.1 = ((f32[32,3,4,8,128]{4,3,2,1,0:T(8,128)}), f32[32,3,4,8,128]{4,3,2,1,0:T(8,128)}, u32[]{:S(2)}, u32[]{:S(2)}) async-start(f32[32,3,4,8,128]{4,3,2,1,0:T(8,128)} %shard_map.68), calls=%async_computation.1 | async-start | bytes 3145728 | tf_op jit(solution)/shard_map/all_to_all | solution.py:255
  52.0 1.0 %shard_map.70 = (f32[4,8,8,128]{3,2,1,0:T(8,128)S(1)}, f32[4,8,8,128]{3,2,1,0:T(8,128)S(1)}) custom-call(s32[1]{0:T(128)} %bitcast.6.x_ref, s32[1]{0:T(128)} %bitcast.yc_ref, s32[1]{0:T(128)} %bitcast.7.zlo_ref, s32[1,3]{1,0:T(1,128)S(1)} %copy-done.4, s32[1,3]{1,0:T(1,128)S(1)} %collective-permute-done.m1, s32[1,3]{1,0:T(1,128)S(1)} %collective-permute-done.1.m2, ...), custom_call_target="tpu_custom_call" | custom-call | tf_op jit(solution)/shard_map/pallas_call | solution.py:349
  53.0 3.3 %collective-permute-start.8 = (f32[4,8,8,128]{3,2,1,0:T(8,128)S(1)}, f32[4,8,8,128]{3,2,1,0:T(8,128)S(1)}, u32[]{:S(2)}, u32[]{:S(2)}) collective-permute-start(f32[4,8,8,128]{3,2,1,0:T(8,128)S(1)} %get-tuple-element.49), channel_id=1, source_target_pairs={{0,8},{8,0},{1,9},{9,1},{2,10},{10,2},{3,11},{11,3},{4,12},{12,4},... | collective-permute-start | bytes 393224 | tf_op jit(solution)/shard_map/ppermute | solution.py:356
  56.4 5.4 %collective-permute-done.8.b_ref = f32[4,8,8,128]{3,2,1,0:T(8,128)S(1)} collective-permute-done((f32[4,8,8,128]{3,2,1,0:T(8,128)S(1)}, f32[4,8,8,128]{3,2,1,0:T(8,128)S(1)}, u32[]{:S(2)}, u32[]{:S(2)}) %collective-permute-start.8) | collective-permute-done | bytes 131104 | tf_op jit(solution)/shard_map/ppermute | solution.py:356
  61.9 1.8 %collective-permute-start.10 = (f32[8,8,128]{2,1,0:T(8,128)S(1)}, f32[8,8,128]{2,1,0:T(8,128)S(1)}, u32[]{:S(2)}, u32[]{:S(2)}) collective-permute-start(f32[8,8,128]{2,1,0:T(8,128)S(1)} %get-tuple-element.52), channel_id=1, source_target_pairs={{0,128},{64,192},{128,0},{192,64},{1,129},{65,193},{129,1},{193,65... | collective-permute-start | bytes 98312 | tf_op jit(solution)/shard_map/ppermute | solution.py:273
  63.7 1.7 %collective-permute-start.11 = (f32[8,8,128]{2,1,0:T(8,128)S(1)}, f32[8,8,128]{2,1,0:T(8,128)S(1)}, u32[]{:S(2)}, u32[]{:S(2)}) collective-permute-start(f32[8,8,128]{2,1,0:T(8,128)S(1)} %get-tuple-element.53), channel_id=1, source_target_pairs={{0,192},{64,128},{128,64},{192,0},{1,193},{65,129},{129,65},{193,1... | collective-permute-start | bytes 98312 | tf_op jit(solution)/shard_map/ppermute | solution.py:273
  65.4 0.8 collective-permute-done.10.c_ref
  66.2 2.4 %collective-permute-done.11.d_ref = f32[8,8,128]{2,1,0:T(8,128)S(1)} collective-permute-done((f32[8,8,128]{2,1,0:T(8,128)S(1)}, f32[8,8,128]{2,1,0:T(8,128)S(1)}, u32[]{:S(2)}, u32[]{:S(2)}) %collective-permute-start.11) | collective-permute-done | bytes 32800 | tf_op jit(solution)/shard_map/ppermute | solution.py:273
  68.7 6.0 %all-to-all-done.1.far = f32[32,3,4,8,128]{4,3,2,1,0:T(8,128)} async-done(((f32[32,3,4,8,128]{4,3,2,1,0:T(8,128)}), f32[32,3,4,8,128]{4,3,2,1,0:T(8,128)}, u32[]{:S(2)}, u32[]{:S(2)}) %all-to-all-start.1) | async-done | bytes 1572896 | tf_op jit(solution)/shard_map/all_to_all | solution.py:255
  74.7 5.4 %shard_map.69 = f32[16,64,128]{2,1,0:T(8,128)} custom-call(s32[128]{0:T(128)S(1)} %bitcast.15, s32[128]{0:T(128)S(1)} %bitcast.17, s32[1]{0:T(128)} %bitcast.10.count, f32[128,128,128]{2,1,0:T(8,128)} %bitcast.19, f32[64,2048]{1,0:T(8,128)S(1)} %bitcast.13, f32[32,3,4,8,128]{4,3,2,1,0:T(8,128)} %all-to-all-done.1.far, f32[16,64,128]{2,1,0:T(8,128)S(1)} %copy-done.1), custom_call_target="tpu_custom_call" | custom-call | flops 805306368 | bytes 8388608 | tf_op jit(solution)/shard_map/pallas_call | solution.py:360
  80.1 4.3 %all-to-all-start.2 = ((f32[16,64,128]{2,1,0:T(8,128)}), f32[16,64,128]{2,1,0:T(8,128)S(1)}, u32[]{:S(2)}, u32[]{:S(2)}) async-start(f32[16,64,128]{2,1,0:T(8,128)} %shard_map.69), calls=%async_computation.2 | async-start | bytes 1048576 | tf_op jit(solution)/shard_map/all_to_all | solution.py:255
  84.4 0.8 collective-permute-start.12
  85.2 1.2 %collective-permute-start.13 = (f32[8,128]{1,0:T(8,128)S(1)}, f32[8,128]{1,0:T(8,128)S(1)}, u32[]{:S(2)}, u32[]{:S(2)}) collective-permute-start(f32[8,128]{1,0:T(8,128)S(1)} %get-tuple-element.65), channel_id=1, source_target_pairs={{0,2},{1,3},{2,0},{3,1},{4,6},{5,7},{6,4},{7,5},{8,10},{9,11},{10,... | collective-permute-start | bytes 12296 | tf_op jit(solution)/shard_map/ppermute | solution.py:273
  86.4 0.5 collective-permute-start.14
  86.9 3.1 %collective-permute-start.15 = (f32[8,128]{1,0:T(8,128)S(1)}, f32[8,128]{1,0:T(8,128)S(1)}, u32[]{:S(2)}, u32[]{:S(2)}) collective-permute-start(f32[8,128]{1,0:T(8,128)S(1)} %get-tuple-element.67), channel_id=1, source_target_pairs={{0,4},{1,5},{2,6},{3,7},{4,0},{5,1},{6,2},{7,3},{8,12},{9,13},{10,... | collective-permute-start | bytes 12296 | tf_op jit(solution)/shard_map/ppermute | solution.py:273
  90.2 3.5 %collective-permute-start.17 = (f32[8,128]{1,0:T(8,128)S(1)}, f32[8,128]{1,0:T(8,128)S(1)}, u32[]{:S(2)}, u32[]{:S(2)}) collective-permute-start(f32[8,128]{1,0:T(8,128)S(1)} %get-tuple-element.69), channel_id=1, source_target_pairs={{0,6},{1,7},{2,4},{3,5},{4,2},{5,3},{6,0},{7,1},{8,14},{9,15},{10,... | collective-permute-start | bytes 12296 | tf_op jit(solution)/shard_map/ppermute | solution.py:273
  93.8 0.9 collective-permute-done.16.refs_5_
  94.8 3.5 %collective-permute-done.18.refs_7_ = f32[8,128]{1,0:T(8,128)S(1)} collective-permute-done((f32[8,128]{1,0:T(8,128)S(1)}, f32[8,128]{1,0:T(8,128)S(1)}, u32[]{:S(2)}, u32[]{:S(2)}) %collective-permute-start.18) | collective-permute-done | bytes 4128 | tf_op jit(solution)/shard_map/ppermute | solution.py:273
  98.5 0.7 shard_map.73
  (32 shorter events, 1.4 us)
Async XLA Ops:
  6.4 8.8 %copy-start = (f32[1,64,2048]{2,1,0:T(8,128)S(1)}, f32[1,64,2048]{2,1,0:T(8,128)}, u32[]{:S(2)}) copy-start(f32[1,64,2048]{2,1,0:T(8,128)} %param.6) | copy-start | bytes 1572868
  6.4 27.6 %copy-start.4 = (s32[1,3]{1,0:T(1,128)S(1)}, s32[1,3]{1,0:T(1,128)}, u32[]{:S(2)}) copy-start(s32[1,3]{1,0:T(1,128)} %m0.3) | copy-start | bytes 40
  6.4 36.0 %all-to-all-start = ((f32[32,3,4,8,128]{4,3,2,1,0:T(8,128)}), f32[32,3,4,8,128]{4,3,2,1,0:T(8,128)S(1)}, u32[]{:S(2)}, u32[]{:S(2)}) async-start(f32[32,3,4,8,128]{4,3,2,1,0:T(8,128)} %get-tuple-element.38), calls=%async_computation | async-start | bytes 3145728 | tf_op jit(solution)/shard_map/all_to_all | solution.py:255
  15.3 12.9 %collective-permute-start.3 = (f32[8,4,8,128]{3,2,1,0:T(8,128)S(1)}, f32[8,4,8,128]{3,2,1,0:T(8,128)S(1)}, u32[]{:S(2)}, u32[]{:S(2)}) collective-permute-start(f32[8,4,8,128]{3,2,1,0:T(8,128)S(1)} %shard_map.65.near_ref), channel_id=1, source_target_pairs={{0,200},{8,192},{64,136},{72,128},{128,72},{136,64},{192,8},{200,0... | collective-permute-start | bytes 393224 | tf_op jit(solution)/shard_map/ppermute | solution.py:309
  28.2 1.9 %collective-permute-start.4 = (f32[4,2,4,8,128]{4,3,2,1,0:T(8,128)S(1)}, f32[4,2,4,8,128]{4,3,2,1,0:T(8,128)S(1)}, u32[]{:S(2)}, u32[]{:S(2)}) collective-permute-start(f32[4,2,4,8,128]{4,3,2,1,0:T(8,128)S(1)} %get-tuple-element.40), channel_id=1, source_target_pairs={{0,1},{1,0},{2,3},{3,2},{4,5},{5,4},{6,7},{7,6},{8,9},{9,8},{10,11... | collective-permute-start | bytes 393224 | tf_op jit(solution)/shard_map/ppermute | solution.py:331
  30.1 10.5 %collective-permute-start.5 = (f32[2,2,4,8,128]{4,3,2,1,0:T(8,128)S(1)}, f32[2,2,4,8,128]{4,3,2,1,0:T(8,128)S(1)}, u32[]{:S(2)}, u32[]{:S(2)}) collective-permute-start(f32[2,2,4,8,128]{4,3,2,1,0:T(8,128)S(1)} %get-tuple-element.42), channel_id=1, source_target_pairs={{0,2},{2,0},{4,6},{6,4},{1,3},{3,1},{5,7},{7,5},{8,10},{10,8},{12,... | collective-permute-start | bytes 196616 | tf_op jit(solution)/shard_map/ppermute | solution.py:273
  31.5 9.0 %collective-permute-start.6 = (f32[2,2,4,8,128]{4,3,2,1,0:T(8,128)S(1)}, f32[2,2,4,8,128]{4,3,2,1,0:T(8,128)S(1)}, u32[]{:S(2)}, u32[]{:S(2)}) collective-permute-start(f32[2,2,4,8,128]{4,3,2,1,0:T(8,128)S(1)} %get-tuple-element.43), channel_id=1, source_target_pairs={{0,4},{2,6},{4,0},{6,2},{1,5},{3,7},{5,1},{7,3},{8,12},{10,14},{12... | collective-permute-start | bytes 196616 | tf_op jit(solution)/shard_map/ppermute | solution.py:273
  33.9 6.6 %collective-permute-start.7 = (f32[2,2,4,8,128]{4,3,2,1,0:T(8,128)S(1)}, f32[2,2,4,8,128]{4,3,2,1,0:T(8,128)S(1)}, u32[]{:S(2)}, u32[]{:S(2)}) collective-permute-start(f32[2,2,4,8,128]{4,3,2,1,0:T(8,128)S(1)} %get-tuple-element.44), channel_id=1, source_target_pairs={{0,6},{2,4},{4,2},{6,0},{1,7},{3,5},{5,3},{7,1},{8,14},{10,12},{12... | collective-permute-start | bytes 196616 | tf_op jit(solution)/shard_map/ppermute | solution.py:273
  34.0 3.8 %collective-permute-start.2 = (s32[1,3]{1,0:T(1,128)S(1)}, s32[1,3]{1,0:T(1,128)S(1)}, u32[]{:S(2)}, u32[]{:S(2)}) collective-permute-start(s32[1,3]{1,0:T(1,128)S(1)} %copy-done.4), channel_id=1, source_target_pairs={{0,16},{16,32},{32,48},{48,0},{1,17},{17,33},{33,49},{49,1},{2,18}... | collective-permute-start | bytes 44 | tf_op jit(solution)/shard_map/ppermute | solution.py:311
  35.4 4.2 %collective-permute-start.1 = (s32[1,3]{1,0:T(1,128)S(1)}, s32[1,3]{1,0:T(1,128)S(1)}, u32[]{:S(2)}, u32[]{:S(2)}) collective-permute-start(s32[1,3]{1,0:T(1,128)S(1)} %copy-done.4), channel_id=1, source_target_pairs={{0,32},{16,48},{32,0},{48,16},{1,33},{17,49},{33,1},{49,17},{2,34}... | collective-permute-start | bytes 44 | tf_op jit(solution)/shard_map/ppermute | solution.py:311
  37.8 2.7 %collective-permute-start = (s32[1,3]{1,0:T(1,128)S(1)}, s32[1,3]{1,0:T(1,128)S(1)}, u32[]{:S(2)}, u32[]{:S(2)}) collective-permute-start(s32[1,3]{1,0:T(1,128)S(1)} %copy-done.4), channel_id=1, source_target_pairs={{0,48},{16,0},{32,16},{48,32},{1,49},{17,1},{33,17},{49,33},{2,50}... | collective-permute-start | bytes 44 | tf_op jit(solution)/shard_map/ppermute | solution.py:311
  42.4 32.3 %all-to-all-start.1 = ((f32[32,3,4,8,128]{4,3,2,1,0:T(8,128)}), f32[32,3,4,8,128]{4,3,2,1,0:T(8,128)}, u32[]{:S(2)}, u32[]{:S(2)}) async-start(f32[32,3,4,8,128]{4,3,2,1,0:T(8,128)} %shard_map.68), calls=%async_computation.1 | async-start | bytes 3145728 | tf_op jit(solution)/shard_map/all_to_all | solution.py:255
  52.0 22.7 %copy-start.1 = (f32[16,64,128]{2,1,0:T(8,128)S(1)}, f32[16,64,128]{2,1,0:T(8,128)}, u32[]{:S(2)}) copy-start(f32[16,64,128]{2,1,0:T(8,128)} %get-tuple-element.46.mine) | copy-start | bytes 1572868
  52.0 22.7 %copy-start.2 = (s32[1,1,128]{2,1,0:T(1,128)S(1)}, s32[1,1,128]{2,1,0:T(1,128)}, u32[]{:S(2)}) copy-start(s32[1,1,128]{2,1,0:T(1,128)} %param.8) | copy-start | bytes 1540
  52.0 22.7 %copy-start.3 = (s32[1,1,128]{2,1,0:T(1,128)S(1)}, s32[1,1,128]{2,1,0:T(1,128)}, u32[]{:S(2)}) copy-start(s32[1,1,128]{2,1,0:T(1,128)} %param.9) | copy-start | bytes 1540
  53.0 8.7 %collective-permute-start.8 = (f32[4,8,8,128]{3,2,1,0:T(8,128)S(1)}, f32[4,8,8,128]{3,2,1,0:T(8,128)S(1)}, u32[]{:S(2)}, u32[]{:S(2)}) collective-permute-start(f32[4,8,8,128]{3,2,1,0:T(8,128)S(1)} %get-tuple-element.49), channel_id=1, source_target_pairs={{0,8},{8,0},{1,9},{9,1},{2,10},{10,2},{3,11},{11,3},{4,12},{12,4},... | collective-permute-start | bytes 393224 | tf_op jit(solution)/shard_map/ppermute | solution.py:356
  61.8 3.6 %collective-permute-start.9 = (f32[8,8,128]{2,1,0:T(8,128)S(1)}, f32[8,8,128]{2,1,0:T(8,128)S(1)}, u32[]{:S(2)}, u32[]{:S(2)}) collective-permute-start(f32[8,8,128]{2,1,0:T(8,128)S(1)} %get-tuple-element.51), channel_id=1, source_target_pairs={{0,64},{64,0},{128,192},{192,128},{1,65},{65,1},{129,193},{193,129... | collective-permute-start | bytes 98312 | tf_op jit(solution)/shard_map/ppermute | solution.py:273
  61.9 4.3 %collective-permute-start.10 = (f32[8,8,128]{2,1,0:T(8,128)S(1)}, f32[8,8,128]{2,1,0:T(8,128)S(1)}, u32[]{:S(2)}, u32[]{:S(2)}) collective-permute-start(f32[8,8,128]{2,1,0:T(8,128)S(1)} %get-tuple-element.52), channel_id=1, source_target_pairs={{0,128},{64,192},{128,0},{192,64},{1,129},{65,193},{129,1},{193,65... | collective-permute-start | bytes 98312 | tf_op jit(solution)/shard_map/ppermute | solution.py:273
  63.7 5.0 %collective-permute-start.11 = (f32[8,8,128]{2,1,0:T(8,128)S(1)}, f32[8,8,128]{2,1,0:T(8,128)S(1)}, u32[]{:S(2)}, u32[]{:S(2)}) collective-permute-start(f32[8,8,128]{2,1,0:T(8,128)S(1)} %get-tuple-element.53), channel_id=1, source_target_pairs={{0,192},{64,128},{128,64},{192,0},{1,193},{65,129},{129,65},{193,1... | collective-permute-start | bytes 98312 | tf_op jit(solution)/shard_map/ppermute | solution.py:273
  80.1 18.4 %all-to-all-start.2 = ((f32[16,64,128]{2,1,0:T(8,128)}), f32[16,64,128]{2,1,0:T(8,128)S(1)}, u32[]{:S(2)}, u32[]{:S(2)}) async-start(f32[16,64,128]{2,1,0:T(8,128)} %shard_map.69), calls=%async_computation.2 | async-start | bytes 1048576 | tf_op jit(solution)/shard_map/all_to_all | solution.py:255
  84.4 5.8 %collective-permute-start.12 = (f32[8,128]{1,0:T(8,128)S(1)}, f32[8,128]{1,0:T(8,128)S(1)}, u32[]{:S(2)}, u32[]{:S(2)}) collective-permute-start(f32[8,128]{1,0:T(8,128)S(1)} %get-tuple-element.64), channel_id=1, source_target_pairs={{0,1},{1,0},{2,3},{3,2},{4,5},{5,4},{6,7},{7,6},{8,9},{9,8},{10,11... | collective-permute-start | bytes 12296 | tf_op jit(solution)/shard_map/ppermute | solution.py:273
  85.2 8.6 %collective-permute-start.13 = (f32[8,128]{1,0:T(8,128)S(1)}, f32[8,128]{1,0:T(8,128)S(1)}, u32[]{:S(2)}, u32[]{:S(2)}) collective-permute-start(f32[8,128]{1,0:T(8,128)S(1)} %get-tuple-element.65), channel_id=1, source_target_pairs={{0,2},{1,3},{2,0},{3,1},{4,6},{5,7},{6,4},{7,5},{8,10},{9,11},{10,... | collective-permute-start | bytes 12296 | tf_op jit(solution)/shard_map/ppermute | solution.py:273
  86.4 7.5 %collective-permute-start.14 = (f32[8,128]{1,0:T(8,128)S(1)}, f32[8,128]{1,0:T(8,128)S(1)}, u32[]{:S(2)}, u32[]{:S(2)}) collective-permute-start(f32[8,128]{1,0:T(8,128)S(1)} %get-tuple-element.66), channel_id=1, source_target_pairs={{0,3},{1,2},{2,1},{3,0},{4,7},{5,6},{6,5},{7,4},{8,11},{9,10},{10,... | collective-permute-start | bytes 12296 | tf_op jit(solution)/shard_map/ppermute | solution.py:273
  86.9 6.9 %collective-permute-start.15 = (f32[8,128]{1,0:T(8,128)S(1)}, f32[8,128]{1,0:T(8,128)S(1)}, u32[]{:S(2)}, u32[]{:S(2)}) collective-permute-start(f32[8,128]{1,0:T(8,128)S(1)} %get-tuple-element.67), channel_id=1, source_target_pairs={{0,4},{1,5},{2,6},{3,7},{4,0},{5,1},{6,2},{7,3},{8,12},{9,13},{10,... | collective-permute-start | bytes 12296 | tf_op jit(solution)/shard_map/ppermute | solution.py:273
  90.0 4.8 %collective-permute-start.16 = (f32[8,128]{1,0:T(8,128)S(1)}, f32[8,128]{1,0:T(8,128)S(1)}, u32[]{:S(2)}, u32[]{:S(2)}) collective-permute-start(f32[8,128]{1,0:T(8,128)S(1)} %get-tuple-element.68), channel_id=1, source_target_pairs={{0,5},{1,4},{2,7},{3,6},{4,1},{5,0},{6,3},{7,2},{8,13},{9,12},{10,... | collective-permute-start | bytes 12296 | tf_op jit(solution)/shard_map/ppermute | solution.py:273
  90.2 4.6 %collective-permute-start.17 = (f32[8,128]{1,0:T(8,128)S(1)}, f32[8,128]{1,0:T(8,128)S(1)}, u32[]{:S(2)}, u32[]{:S(2)}) collective-permute-start(f32[8,128]{1,0:T(8,128)S(1)} %get-tuple-element.69), channel_id=1, source_target_pairs={{0,6},{1,7},{2,4},{3,5},{4,2},{5,3},{6,0},{7,1},{8,14},{9,15},{10,... | collective-permute-start | bytes 12296 | tf_op jit(solution)/shard_map/ppermute | solution.py:273
  93.8 4.5 %collective-permute-start.18 = (f32[8,128]{1,0:T(8,128)S(1)}, f32[8,128]{1,0:T(8,128)S(1)}, u32[]{:S(2)}, u32[]{:S(2)}) collective-permute-start(f32[8,128]{1,0:T(8,128)S(1)} %get-tuple-element.70), channel_id=1, source_target_pairs={{0,7},{1,6},{2,5},{3,4},{4,3},{5,2},{6,1},{7,0},{8,15},{9,14},{10,... | collective-permute-start | bytes 12296 | tf_op jit(solution)/shard_map/ppermute | solution.py:273

commit v4 on v3

--- a/solution.py
+++ b/solution.py
@@ -128,16 +128,18 @@
         outs[step][...] = a_ref[step] + b_ref[step]
 
 
-def add_zlo_kernel(a_ref, b_ref, c_ref, d_ref, *outs):
-    for step in range(YC):
-        outs[step][...] = (a_ref[step] + b_ref[step]) + (c_ref[step] + d_ref[step])
+def add_zlo_kernel(a_ref, b_ref, c_ref, d_ref, same_ref, cross_ref):
+    for step in range(Y):
+        for core, out_ref in enumerate((same_ref, cross_ref)):
+            at = step * CORE + core
+            out_ref[step] = (a_ref[at] + b_ref[at]) + (c_ref[at] + d_ref[at])
 
 
 def final_kernel(yc_ref, rows_ref, *refs):
-    parts, out_ref = refs[:YC], refs[YC]
+    parts, out_ref = refs[:Y], refs[Y]
     for step in range(YC):
         at = pl.ds(pl.multiple_of((yc_ref[0] ^ step) * SUB, SUB), SUB)
-        total = parts[step][...]
+        total = parts[step // CORE][step % CORE]
         for group in range(rows_ref.shape[0]):
             total = total + rows_ref[group, at]
         out_ref[at] = total
@@ -356,7 +358,8 @@
     other = lax.ppermute(other, "zhi", [(0, 1), (1, 0)])
     parts = local(add_zhi_kernel, [spread[1:]] * ZLO, [VMEM] * 2, limit=SMALL)(near, other)
     parts = swaps(parts, "zlo", ZLO)
-    parts = local(add_zlo_kernel, [spread[2:]] * YC, [VMEM] * ZLO, limit=SMALL)(*parts)
+    side = (Y, SUB, LANE)
+    parts = local(add_zlo_kernel, [side] * CORE, [VMEM] * ZLO, limit=SMALL)(*parts)
     (rows,) = local(
         rows_kernel,
         [(blocks, vecs, LANE)],
@@ -367,8 +370,10 @@
     )(*ids, tile_set, own, far, mine)
     rows, *parts = lax.optimization_barrier((rows, *parts))
     rows = exchange(rows, GRP_AXES)
-    parts = swaps(parts, YC_AXES, YC)
-    (total,) = local(final_kernel, [(vecs, LANE)], [SMEM] + [VMEM] * (1 + YC), limit=SMALL)(
+    cross = lax.ppermute(parts[1], "core", [(0, 1), (1, 0)])
+    parts = local(join_kernel, [(CORE, SUB, LANE)] * Y, [VMEM] * 2, limit=SMALL)(parts[0], cross)
+    parts = swaps(parts, "y", Y)
+    (total,) = local(final_kernel, [(vecs, LANE)], [SMEM] + [VMEM] * (1 + Y), limit=SMALL)(
         yc, rows, *parts
     )
     return total[None]

time: 99.7 us -> 99.7 us (level)
  waiting for transfers between devices: 28.2 us -> 32.1 us
  starting transfers between devices: 55.3 us -> 51.4 us
    ppermute x13 -> x9, starting transfers between devices: 17 us -> 12.3 us  [swaps(): lax.ppermute(arrays[step], axes, [(i, i ^ step) for i in range(count)])]
    all_to_all x3, waiting for transfers between devices: 6.17 us -> 9.68 us  [exchange(): return lax.all_to_all(value, axes, 0, 0, tiled=False)]
    ppermute x13 -> x9, waiting for transfers between devices: 7.69 us -> 7.23 us  [swaps(): lax.ppermute(arrays[step], axes, [(i, i ^ step) for i in range(count)])]
  transfers between devices with their start and end apart: 22 -> 19, of which waited for: 11 -> 12; matrix products, arithmetic and copies ran while one was open for 0% -> 0% of each run, Pallas kernels for 3% -> 3%
where the time goes in v4:
time: 99.7 us; the launch traced here: 99.1 us
  starting transfers between devices  51.4 us (52%)
  waiting for transfers between devices  32.1 us (32%)
  Pallas kernels  14.8 us (15%)
    all_to_all x3, starting transfers between devices, exchange(): return lax.all_to_all(value, axes, 0, 0, tiled=False)  22.6 us
    ppermute x9, starting transfers between devices, swaps(): lax.ppermute(arrays[step], axes, [(i, i ^ step) for i in range(count)])  12.3 us
    all_to_all x3, waiting for transfers between devices, exchange(): return lax.all_to_all(value, axes, 0, 0, tiled=False)  9.68 us
    ppermute x9, waiting for transfers between devices, swaps(): lax.ppermute(arrays[step], axes, [(i, i ^ step) for i in range(count)])  7.23 us
    ppermute x1, waiting for transfers between devices, on_device(): lax.ppermute(near, ('zlo', 'zhi'), [(i, ZLO * ZHI - 1 - i) for i in range...  6.45 us
    ppermute x1, starting transfers between devices, on_device(): lax.ppermute(near, ('zlo', 'zhi'), [(i, ZLO * ZHI - 1 - i) for i in range...  6.44 us
    pallas_call x1, Pallas kernels, on_device(): local(columns_kernel, [(FAN, REGIONS - 1, *piece), (blocks, vecs, LANE)],...  5.74 us
    ppermute x1, waiting for transfers between devices, on_device(): other = lax.ppermute(other, 'zhi', [(0, 1), (1, 0)])  5.43 us
  transfers between devices with their start and end apart: 19, of which 12 were waited for; matrix products, arithmetic and copies ran while one was open for 0% of the time, Pallas kernels for 3%

profile of v4, /device:TPU:1, one launch (start us, length us, event | category | flops | bytes accessed | tf_op | source)
XLA Modules:
  0.0 99.1 jit_solution(5667909292074751865)
XLA Ops:
  0.7 5.7 %shard_map.64 = (f32[32,3,4,8,128]{4,3,2,1,0:T(8,128)}, f32[16,64,128]{2,1,0:T(8,128)}) custom-call(s32[128]{0:T(128)} %bitcast.14, s32[128]{0:T(128)} %bitcast.16, s32[1]{0:T(128)} %bitcast.9.count, f32[128,128,128]{2,1,0:T(8,128)} %bitcast.18, f32[64,2048]{1,0:T(8,128)} %bitcast.11), custom_call_target="tpu_custom_call" | custom-call | flops 805306368 | bytes 8388608 | tf_op jit(solution)/shard_map/pallas_call | solution.py:316
  6.4 8.7 %all-to-all-start = ((f32[32,3,4,8,128]{4,3,2,1,0:T(8,128)}), f32[32,3,4,8,128]{4,3,2,1,0:T(8,128)S(1)}, u32[]{:S(2)}, u32[]{:S(2)}) async-start(f32[32,3,4,8,128]{4,3,2,1,0:T(8,128)} %get-tuple-element.30), calls=%async_computation | async-start | bytes 3145728 | tf_op jit(solution)/shard_map/all_to_all | solution.py:257
  15.3 6.4 %collective-permute-start.3 = (f32[8,4,8,128]{3,2,1,0:T(8,128)S(1)}, f32[8,4,8,128]{3,2,1,0:T(8,128)S(1)}, u32[]{:S(2)}, u32[]{:S(2)}) collective-permute-start(f32[8,4,8,128]{3,2,1,0:T(8,128)S(1)} %shard_map.65.near_ref), channel_id=1, source_target_pairs={{0,200},{8,192},{64,136},{72,128},{128,72},{136,64},{192,8},{200,0... | collective-permute-start | bytes 393224 | tf_op jit(solution)/shard_map/ppermute | solution.py:311
  21.7 6.4 %collective-permute-done.3.other_ref = f32[8,4,8,128]{3,2,1,0:T(8,128)S(1)} collective-permute-done((f32[8,4,8,128]{3,2,1,0:T(8,128)S(1)}, f32[8,4,8,128]{3,2,1,0:T(8,128)S(1)}, u32[]{:S(2)}, u32[]{:S(2)}) %collective-permute-start.3) | collective-permute-done | bytes 131104 | tf_op jit(solution)/shard_map/ppermute | solution.py:311
  28.2 0.9 collective-permute-start.4
  29.1 1.0 collective-permute-done.4.cross_ref
  30.1 1.4 %collective-permute-start.5 = (f32[2,2,4,8,128]{4,3,2,1,0:T(8,128)S(1)}, f32[2,2,4,8,128]{4,3,2,1,0:T(8,128)S(1)}, u32[]{:S(2)}, u32[]{:S(2)}) collective-permute-start(f32[2,2,4,8,128]{4,3,2,1,0:T(8,128)S(1)} %get-tuple-element.34), channel_id=1, source_target_pairs={{0,2},{2,0},{4,6},{6,4},{1,3},{3,1},{5,7},{7,5},{8,10},{10,8},{12,... | collective-permute-start | bytes 196616 | tf_op jit(solution)/shard_map/ppermute | solution.py:275
  31.5 2.4 %collective-permute-start.6 = (f32[2,2,4,8,128]{4,3,2,1,0:T(8,128)S(1)}, f32[2,2,4,8,128]{4,3,2,1,0:T(8,128)S(1)}, u32[]{:S(2)}, u32[]{:S(2)}) collective-permute-start(f32[2,2,4,8,128]{4,3,2,1,0:T(8,128)S(1)} %get-tuple-element.35), channel_id=1, source_target_pairs={{0,4},{2,6},{4,0},{6,2},{1,5},{3,7},{5,1},{7,3},{8,12},{10,14},{12... | collective-permute-start | bytes 196616 | tf_op jit(solution)/shard_map/ppermute | solution.py:275
  34.0 1.4 %collective-permute-start.2 = (s32[1,3]{1,0:T(1,128)S(1)}, s32[1,3]{1,0:T(1,128)S(1)}, u32[]{:S(2)}, u32[]{:S(2)}) collective-permute-start(s32[1,3]{1,0:T(1,128)S(1)} %copy-done.4), channel_id=1, source_target_pairs={{0,16},{16,32},{32,48},{48,0},{1,17},{17,33},{33,49},{49,1},{2,18}... | collective-permute-start | bytes 44 | tf_op jit(solution)/shard_map/ppermute | solution.py:313
  35.4 2.4 %collective-permute-start.1 = (s32[1,3]{1,0:T(1,128)S(1)}, s32[1,3]{1,0:T(1,128)S(1)}, u32[]{:S(2)}, u32[]{:S(2)}) collective-permute-start(s32[1,3]{1,0:T(1,128)S(1)} %copy-done.4), channel_id=1, source_target_pairs={{0,32},{16,48},{32,0},{48,16},{1,33},{17,49},{33,1},{49,17},{2,34}... | collective-permute-start | bytes 44 | tf_op jit(solution)/shard_map/ppermute | solution.py:313
  37.8 1.2 %collective-permute-start = (s32[1,3]{1,0:T(1,128)S(1)}, s32[1,3]{1,0:T(1,128)S(1)}, u32[]{:S(2)}, u32[]{:S(2)}) collective-permute-start(s32[1,3]{1,0:T(1,128)S(1)} %copy-done.4), channel_id=1, source_target_pairs={{0,48},{16,0},{32,16},{48,32},{1,49},{17,1},{33,17},{49,33},{2,50}... | collective-permute-start | bytes 44 | tf_op jit(solution)/shard_map/ppermute | solution.py:313
  39.6 0.9 collective-permute-done.m1
  40.6 1.8 %shard_map.68 = f32[32,3,4,8,128]{4,3,2,1,0:T(8,128)} custom-call(s32[1]{0:T(128)} %bitcast.6.x_ref, s32[1]{0:T(128)} %bitcast.yc_ref, s32[1,3]{1,0:T(1,128)S(1)} %copy-done.4, s32[1,3]{1,0:T(1,128)S(1)} %collective-permute-done.m1, s32[1,3]{1,0:T(1,128)S(1)} %collective-permute-done.1.m2, s32[1,3]{1,0:T(1,128)S(1)} %collective-permute-done.2.m3, ...), custom_call_target="tpu_custom_call" | custom-call | tf_op jit(solution)/shard_map/pallas_call | solution.py:336
  42.4 9.6 %all-to-all-start.1 = ((f32[32,3,4,8,128]{4,3,2,1,0:T(8,128)}), f32[32,3,4,8,128]{4,3,2,1,0:T(8,128)}, u32[]{:S(2)}, u32[]{:S(2)}) async-start(f32[32,3,4,8,128]{4,3,2,1,0:T(8,128)} %shard_map.68), calls=%async_computation.1 | async-start | bytes 3145728 | tf_op jit(solution)/shard_map/all_to_all | solution.py:257
  52.0 1.0 %shard_map.70 = (f32[4,8,8,128]{3,2,1,0:T(8,128)S(1)}, f32[4,8,8,128]{3,2,1,0:T(8,128)S(1)}) custom-call(s32[1]{0:T(128)} %bitcast.6.x_ref, s32[1]{0:T(128)} %bitcast.yc_ref, s32[1]{0:T(128)} %bitcast.7.zlo_ref, s32[1,3]{1,0:T(1,128)S(1)} %copy-done.4, s32[1,3]{1,0:T(1,128)S(1)} %collective-permute-done.m1, s32[1,3]{1,0:T(1,128)S(1)} %collective-permute-done.1.m2, ...), custom_call_target="tpu_custom_call" | custom-call | tf_op jit(solution)/shard_map/pallas_call | solution.py:351
  53.0 3.3 %collective-permute-start.8 = (f32[4,8,8,128]{3,2,1,0:T(8,128)S(1)}, f32[4,8,8,128]{3,2,1,0:T(8,128)S(1)}, u32[]{:S(2)}, u32[]{:S(2)}) collective-permute-start(f32[4,8,8,128]{3,2,1,0:T(8,128)S(1)} %get-tuple-element.41), channel_id=1, source_target_pairs={{0,8},{8,0},{1,9},{9,1},{2,10},{10,2},{3,11},{11,3},{4,12},{12,4},... | collective-permute-start | bytes 393224 | tf_op jit(solution)/shard_map/ppermute | solution.py:358
  56.4 5.4 %collective-permute-done.8.b_ref = f32[4,8,8,128]{3,2,1,0:T(8,128)S(1)} collective-permute-done((f32[4,8,8,128]{3,2,1,0:T(8,128)S(1)}, f32[4,8,8,128]{3,2,1,0:T(8,128)S(1)}, u32[]{:S(2)}, u32[]{:S(2)}) %collective-permute-start.8) | collective-permute-done | bytes 131104 | tf_op jit(solution)/shard_map/ppermute | solution.py:358
  61.9 1.8 %collective-permute-start.10 = (f32[8,8,128]{2,1,0:T(8,128)S(1)}, f32[8,8,128]{2,1,0:T(8,128)S(1)}, u32[]{:S(2)}, u32[]{:S(2)}) collective-permute-start(f32[8,8,128]{2,1,0:T(8,128)S(1)} %get-tuple-element.44), channel_id=1, source_target_pairs={{0,128},{64,192},{128,0},{192,64},{1,129},{65,193},{129,1},{193,65... | collective-permute-start | bytes 98312 | tf_op jit(solution)/shard_map/ppermute | solution.py:275
  63.7 1.7 %collective-permute-start.11 = (f32[8,8,128]{2,1,0:T(8,128)S(1)}, f32[8,8,128]{2,1,0:T(8,128)S(1)}, u32[]{:S(2)}, u32[]{:S(2)}) collective-permute-start(f32[8,8,128]{2,1,0:T(8,128)S(1)} %get-tuple-element.45), channel_id=1, source_target_pairs={{0,192},{64,128},{128,64},{192,0},{1,193},{65,129},{129,65},{193,1... | collective-permute-start | bytes 98312 | tf_op jit(solution)/shard_map/ppermute | solution.py:275
  65.4 0.8 collective-permute-done.10.c_ref
  66.2 2.4 %collective-permute-done.11.d_ref = f32[8,8,128]{2,1,0:T(8,128)S(1)} collective-permute-done((f32[8,8,128]{2,1,0:T(8,128)S(1)}, f32[8,8,128]{2,1,0:T(8,128)S(1)}, u32[]{:S(2)}, u32[]{:S(2)}) %collective-permute-start.11) | collective-permute-done | bytes 32800 | tf_op jit(solution)/shard_map/ppermute | solution.py:275
  68.7 6.0 %all-to-all-done.1.far = f32[32,3,4,8,128]{4,3,2,1,0:T(8,128)} async-done(((f32[32,3,4,8,128]{4,3,2,1,0:T(8,128)}), f32[32,3,4,8,128]{4,3,2,1,0:T(8,128)}, u32[]{:S(2)}, u32[]{:S(2)}) %all-to-all-start.1) | async-done | bytes 1572896 | tf_op jit(solution)/shard_map/all_to_all | solution.py:257
  74.7 5.4 %shard_map.69 = f32[16,64,128]{2,1,0:T(8,128)} custom-call(s32[128]{0:T(128)S(1)} %bitcast.15, s32[128]{0:T(128)S(1)} %bitcast.17, s32[1]{0:T(128)} %bitcast.10.count, f32[128,128,128]{2,1,0:T(8,128)} %bitcast.19, f32[64,2048]{1,0:T(8,128)S(1)} %bitcast.13, f32[32,3,4,8,128]{4,3,2,1,0:T(8,128)} %all-to-all-done.1.far, f32[16,64,128]{2,1,0:T(8,128)S(1)} %copy-done.1), custom_call_target="tpu_custom_call" | custom-call | flops 805306368 | bytes 8388608 | tf_op jit(solution)/shard_map/pallas_call | solution.py:363
  80.1 4.3 %all-to-all-start.2 = ((f32[16,64,128]{2,1,0:T(8,128)}), f32[16,64,128]{2,1,0:T(8,128)S(1)}, u32[]{:S(2)}, u32[]{:S(2)}) async-start(f32[16,64,128]{2,1,0:T(8,128)} %shard_map.69), calls=%async_computation.2 | async-start | bytes 1048576 | tf_op jit(solution)/shard_map/all_to_all | solution.py:257
  84.4 0.8 collective-permute-start.12
  85.2 0.8 collective-permute-done.12.cross_ref
  86.0 1.2 %collective-permute-start.13 = (f32[2,8,128]{2,1,0:T(8,128)S(1)}, f32[2,8,128]{2,1,0:T(8,128)S(1)}, u32[]{:S(2)}, u32[]{:S(2)}) collective-permute-start(f32[2,8,128]{2,1,0:T(8,128)S(1)} %get-tuple-element.52), channel_id=1, source_target_pairs={{0,2},{2,0},{4,6},{6,4},{1,3},{3,1},{5,7},{7,5},{8,10},{10,8},{12,... | collective-permute-start | bytes 24584 | tf_op jit(solution)/shard_map/ppermute | solution.py:275
  87.2 3.6 %collective-permute-start.14 = (f32[2,8,128]{2,1,0:T(8,128)S(1)}, f32[2,8,128]{2,1,0:T(8,128)S(1)}, u32[]{:S(2)}, u32[]{:S(2)}) collective-permute-start(f32[2,8,128]{2,1,0:T(8,128)S(1)} %get-tuple-element.53), channel_id=1, source_target_pairs={{0,4},{2,6},{4,0},{6,2},{1,5},{3,7},{5,1},{7,3},{8,12},{10,14},{12... | collective-permute-start | bytes 24584 | tf_op jit(solution)/shard_map/ppermute | solution.py:275
  90.8 1.4 %collective-permute-done.14.refs_2_ = f32[2,8,128]{2,1,0:T(8,128)S(1)} collective-permute-done((f32[2,8,128]{2,1,0:T(8,128)S(1)}, f32[2,8,128]{2,1,0:T(8,128)S(1)}, u32[]{:S(2)}, u32[]{:S(2)}) %collective-permute-start.14) | collective-permute-done | bytes 8224 | tf_op jit(solution)/shard_map/ppermute | solution.py:275
  92.2 2.6 %collective-permute-done.15.refs_3_ = f32[2,8,128]{2,1,0:T(8,128)S(1)} collective-permute-done((f32[2,8,128]{2,1,0:T(8,128)S(1)}, f32[2,8,128]{2,1,0:T(8,128)S(1)}, u32[]{:S(2)}, u32[]{:S(2)}) %collective-permute-start.15) | collective-permute-done | bytes 8224 | tf_op jit(solution)/shard_map/ppermute | solution.py:275
  94.8 3.7 %all-to-all-done.2.rows_ref = f32[16,64,128]{2,1,0:T(8,128)S(1)} async-done(((f32[16,64,128]{2,1,0:T(8,128)}), f32[16,64,128]{2,1,0:T(8,128)S(1)}, u32[]{:S(2)}, u32[]{:S(2)}) %all-to-all-start.2) | async-done | bytes 524320 | tf_op jit(solution)/shard_map/all_to_all | solution.py:257
  98.4 0.7 shard_map.74
  (27 shorter events, 1.0 us)
Async XLA Ops:
  6.4 8.8 %copy-start = (f32[1,64,2048]{2,1,0:T(8,128)S(1)}, f32[1,64,2048]{2,1,0:T(8,128)}, u32[]{:S(2)}) copy-start(f32[1,64,2048]{2,1,0:T(8,128)} %param.6) | copy-start | bytes 1572868
  6.4 27.6 %copy-start.4 = (s32[1,3]{1,0:T(1,128)S(1)}, s32[1,3]{1,0:T(1,128)}, u32[]{:S(2)}) copy-start(s32[1,3]{1,0:T(1,128)} %m0.3) | copy-start | bytes 40
  6.4 35.9 %all-to-all-start = ((f32[32,3,4,8,128]{4,3,2,1,0:T(8,128)}), f32[32,3,4,8,128]{4,3,2,1,0:T(8,128)S(1)}, u32[]{:S(2)}, u32[]{:S(2)}) async-start(f32[32,3,4,8,128]{4,3,2,1,0:T(8,128)} %get-tuple-element.30), calls=%async_computation | async-start | bytes 3145728 | tf_op jit(solution)/shard_map/all_to_all | solution.py:257
  15.3 12.9 %collective-permute-start.3 = (f32[8,4,8,128]{3,2,1,0:T(8,128)S(1)}, f32[8,4,8,128]{3,2,1,0:T(8,128)S(1)}, u32[]{:S(2)}, u32[]{:S(2)}) collective-permute-start(f32[8,4,8,128]{3,2,1,0:T(8,128)S(1)} %shard_map.65.near_ref), channel_id=1, source_target_pairs={{0,200},{8,192},{64,136},{72,128},{128,72},{136,64},{192,8},{200,0... | collective-permute-start | bytes 393224 | tf_op jit(solution)/shard_map/ppermute | solution.py:311
  28.2 1.9 %collective-permute-start.4 = (f32[4,2,4,8,128]{4,3,2,1,0:T(8,128)S(1)}, f32[4,2,4,8,128]{4,3,2,1,0:T(8,128)S(1)}, u32[]{:S(2)}, u32[]{:S(2)}) collective-permute-start(f32[4,2,4,8,128]{4,3,2,1,0:T(8,128)S(1)} %get-tuple-element.32), channel_id=1, source_target_pairs={{0,1},{1,0},{2,3},{3,2},{4,5},{5,4},{6,7},{7,6},{8,9},{9,8},{10,11... | collective-permute-start | bytes 393224 | tf_op jit(solution)/shard_map/ppermute | solution.py:333
  30.1 10.5 %collective-permute-start.5 = (f32[2,2,4,8,128]{4,3,2,1,0:T(8,128)S(1)}, f32[2,2,4,8,128]{4,3,2,1,0:T(8,128)S(1)}, u32[]{:S(2)}, u32[]{:S(2)}) collective-permute-start(f32[2,2,4,8,128]{4,3,2,1,0:T(8,128)S(1)} %get-tuple-element.34), channel_id=1, source_target_pairs={{0,2},{2,0},{4,6},{6,4},{1,3},{3,1},{5,7},{7,5},{8,10},{10,8},{12,... | collective-permute-start | bytes 196616 | tf_op jit(solution)/shard_map/ppermute | solution.py:275
  31.5 9.0 %collective-permute-start.6 = (f32[2,2,4,8,128]{4,3,2,1,0:T(8,128)S(1)}, f32[2,2,4,8,128]{4,3,2,1,0:T(8,128)S(1)}, u32[]{:S(2)}, u32[]{:S(2)}) collective-permute-start(f32[2,2,4,8,128]{4,3,2,1,0:T(8,128)S(1)} %get-tuple-element.35), channel_id=1, source_target_pairs={{0,4},{2,6},{4,0},{6,2},{1,5},{3,7},{5,1},{7,3},{8,12},{10,14},{12... | collective-permute-start | bytes 196616 | tf_op jit(solution)/shard_map/ppermute | solution.py:275
  33.9 6.6 %collective-permute-start.7 = (f32[2,2,4,8,128]{4,3,2,1,0:T(8,128)S(1)}, f32[2,2,4,8,128]{4,3,2,1,0:T(8,128)S(1)}, u32[]{:S(2)}, u32[]{:S(2)}) collective-permute-start(f32[2,2,4,8,128]{4,3,2,1,0:T(8,128)S(1)} %get-tuple-element.36), channel_id=1, source_target_pairs={{0,6},{2,4},{4,2},{6,0},{1,7},{3,5},{5,3},{7,1},{8,14},{10,12},{12... | collective-permute-start | bytes 196616 | tf_op jit(solution)/shard_map/ppermute | solution.py:275
  34.0 3.8 %collective-permute-start.2 = (s32[1,3]{1,0:T(1,128)S(1)}, s32[1,3]{1,0:T(1,128)S(1)}, u32[]{:S(2)}, u32[]{:S(2)}) collective-permute-start(s32[1,3]{1,0:T(1,128)S(1)} %copy-done.4), channel_id=1, source_target_pairs={{0,16},{16,32},{32,48},{48,0},{1,17},{17,33},{33,49},{49,1},{2,18}... | collective-permute-start | bytes 44 | tf_op jit(solution)/shard_map/ppermute | solution.py:313
  35.4 4.2 %collective-permute-start.1 = (s32[1,3]{1,0:T(1,128)S(1)}, s32[1,3]{1,0:T(1,128)S(1)}, u32[]{:S(2)}, u32[]{:S(2)}) collective-permute-start(s32[1,3]{1,0:T(1,128)S(1)} %copy-done.4), channel_id=1, source_target_pairs={{0,32},{16,48},{32,0},{48,16},{1,33},{17,49},{33,1},{49,17},{2,34}... | collective-permute-start | bytes 44 | tf_op jit(solution)/shard_map/ppermute | solution.py:313
  37.8 2.7 %collective-permute-start = (s32[1,3]{1,0:T(1,128)S(1)}, s32[1,3]{1,0:T(1,128)S(1)}, u32[]{:S(2)}, u32[]{:S(2)}) collective-permute-start(s32[1,3]{1,0:T(1,128)S(1)} %copy-done.4), channel_id=1, source_target_pairs={{0,48},{16,0},{32,16},{48,32},{1,49},{17,1},{33,17},{49,33},{2,50}... | collective-permute-start | bytes 44 | tf_op jit(solution)/shard_map/ppermute | solution.py:313
  42.4 32.3 %all-to-all-start.1 = ((f32[32,3,4,8,128]{4,3,2,1,0:T(8,128)}), f32[32,3,4,8,128]{4,3,2,1,0:T(8,128)}, u32[]{:S(2)}, u32[]{:S(2)}) async-start(f32[32,3,4,8,128]{4,3,2,1,0:T(8,128)} %shard_map.68), calls=%async_computation.1 | async-start | bytes 3145728 | tf_op jit(solution)/shard_map/all_to_all | solution.py:257
  52.0 22.7 %copy-start.1 = (f32[16,64,128]{2,1,0:T(8,128)S(1)}, f32[16,64,128]{2,1,0:T(8,128)}, u32[]{:S(2)}) copy-start(f32[16,64,128]{2,1,0:T(8,128)} %get-tuple-element.38.mine) | copy-start | bytes 1572868
  52.0 22.7 %copy-start.2 = (s32[1,1,128]{2,1,0:T(1,128)S(1)}, s32[1,1,128]{2,1,0:T(1,128)}, u32[]{:S(2)}) copy-start(s32[1,1,128]{2,1,0:T(1,128)} %param.8) | copy-start | bytes 1540
  52.0 22.7 %copy-start.3 = (s32[1,1,128]{2,1,0:T(1,128)S(1)}, s32[1,1,128]{2,1,0:T(1,128)}, u32[]{:S(2)}) copy-start(s32[1,1,128]{2,1,0:T(1,128)} %param.9) | copy-start | bytes 1540
  53.0 8.7 %collective-permute-start.8 = (f32[4,8,8,128]{3,2,1,0:T(8,128)S(1)}, f32[4,8,8,128]{3,2,1,0:T(8,128)S(1)}, u32[]{:S(2)}, u32[]{:S(2)}) collective-permute-start(f32[4,8,8,128]{3,2,1,0:T(8,128)S(1)} %get-tuple-element.41), channel_id=1, source_target_pairs={{0,8},{8,0},{1,9},{9,1},{2,10},{10,2},{3,11},{11,3},{4,12},{12,4},... | collective-permute-start | bytes 393224 | tf_op jit(solution)/shard_map/ppermute | solution.py:358
  61.8 3.6 %collective-permute-start.9 = (f32[8,8,128]{2,1,0:T(8,128)S(1)}, f32[8,8,128]{2,1,0:T(8,128)S(1)}, u32[]{:S(2)}, u32[]{:S(2)}) collective-permute-start(f32[8,8,128]{2,1,0:T(8,128)S(1)} %get-tuple-element.43), channel_id=1, source_target_pairs={{0,64},{64,0},{128,192},{192,128},{1,65},{65,1},{129,193},{193,129... | collective-permute-start | bytes 98312 | tf_op jit(solution)/shard_map/ppermute | solution.py:275
  61.9 4.3 %collective-permute-start.10 = (f32[8,8,128]{2,1,0:T(8,128)S(1)}, f32[8,8,128]{2,1,0:T(8,128)S(1)}, u32[]{:S(2)}, u32[]{:S(2)}) collective-permute-start(f32[8,8,128]{2,1,0:T(8,128)S(1)} %get-tuple-element.44), channel_id=1, source_target_pairs={{0,128},{64,192},{128,0},{192,64},{1,129},{65,193},{129,1},{193,65... | collective-permute-start | bytes 98312 | tf_op jit(solution)/shard_map/ppermute | solution.py:275
  63.7 5.0 %collective-permute-start.11 = (f32[8,8,128]{2,1,0:T(8,128)S(1)}, f32[8,8,128]{2,1,0:T(8,128)S(1)}, u32[]{:S(2)}, u32[]{:S(2)}) collective-permute-start(f32[8,8,128]{2,1,0:T(8,128)S(1)} %get-tuple-element.45), channel_id=1, source_target_pairs={{0,192},{64,128},{128,64},{192,0},{1,193},{65,129},{129,65},{193,1... | collective-permute-start | bytes 98312 | tf_op jit(solution)/shard_map/ppermute | solution.py:275
  80.1 18.4 %all-to-all-start.2 = ((f32[16,64,128]{2,1,0:T(8,128)}), f32[16,64,128]{2,1,0:T(8,128)S(1)}, u32[]{:S(2)}, u32[]{:S(2)}) async-start(f32[16,64,128]{2,1,0:T(8,128)} %shard_map.69), calls=%async_computation.2 | async-start | bytes 1048576 | tf_op jit(solution)/shard_map/all_to_all | solution.py:257
  84.4 1.6 %collective-permute-start.12 = (f32[4,8,128]{2,1,0:T(8,128)S(1)}, f32[4,8,128]{2,1,0:T(8,128)S(1)}, u32[]{:S(2)}, u32[]{:S(2)}) collective-permute-start(f32[4,8,128]{2,1,0:T(8,128)S(1)} %get-tuple-element.50), channel_id=1, source_target_pairs={{0,1},{1,0},{2,3},{3,2},{4,5},{5,4},{6,7},{7,6},{8,9},{9,8},{10,11... | collective-permute-start | bytes 49160 | tf_op jit(solution)/shard_map/ppermute | solution.py:373
  86.0 4.8 %collective-permute-start.13 = (f32[2,8,128]{2,1,0:T(8,128)S(1)}, f32[2,8,128]{2,1,0:T(8,128)S(1)}, u32[]{:S(2)}, u32[]{:S(2)}) collective-permute-start(f32[2,8,128]{2,1,0:T(8,128)S(1)} %get-tuple-element.52), channel_id=1, source_target_pairs={{0,2},{2,0},{4,6},{6,4},{1,3},{3,1},{5,7},{7,5},{8,10},{10,8},{12,... | collective-permute-start | bytes 24584 | tf_op jit(solution)/shard_map/ppermute | solution.py:275
  87.2 5.0 %collective-permute-start.14 = (f32[2,8,128]{2,1,0:T(8,128)S(1)}, f32[2,8,128]{2,1,0:T(8,128)S(1)}, u32[]{:S(2)}, u32[]{:S(2)}) collective-permute-start(f32[2,8,128]{2,1,0:T(8,128)S(1)} %get-tuple-element.53), channel_id=1, source_target_pairs={{0,4},{2,6},{4,0},{6,2},{1,5},{3,7},{5,1},{7,3},{8,12},{10,14},{12... | collective-permute-start | bytes 24584 | tf_op jit(solution)/shard_map/ppermute | solution.py:275
  90.8 4.0 %collective-permute-start.15 = (f32[2,8,128]{2,1,0:T(8,128)S(1)}, f32[2,8,128]{2,1,0:T(8,128)S(1)}, u32[]{:S(2)}, u32[]{:S(2)}) collective-permute-start(f32[2,8,128]{2,1,0:T(8,128)S(1)} %get-tuple-element.54), channel_id=1, source_target_pairs={{0,6},{2,4},{4,2},{6,0},{1,7},{3,5},{5,3},{7,1},{8,14},{10,12},{12... | collective-permute-start | bytes 24584 | tf_op jit(solution)/shard_map/ppermute | solution.py:275
